TPU v7x, 256 devices: a whole 4x4x8 slice. The times are simulated.
256 devices in a mesh: section: 16 (over z, core), mp: 8 (over x, y_hi), dp: 2 (over y_lo).
Axes of the slice: x: 4, y: 4 (y_hi: 2, y_lo: 2; y = y_hi * 2 + y_lo), z: 8, core: 2. Of those that a mesh axis runs over, the one named last changes fastest.
Arguments:
- enc_out: bfloat16 [2, 512, 4096], P('dp', 'mp', 'section'), may hold values from -6 to 6
- kv_weight: bfloat16 [16, 4096, 2, 4096], P('section', None, None, 'mp'), may hold values from -0.09375 to 0.09375
- dec_query: bfloat16 [16, 2, 512, 4096], P('section', 'dp', None, 'mp'), may hold values from -120 to 120
- ctx_grad: bfloat16 [16, 2, 512, 4096], P('section', 'dp', None, 'mp'), may hold values from -6 to 6
- enc_seg: int32 [2, 512], P('dp'), may hold values from 0 to 7, never falling along the last dimension, each value on 1 to 128 neighbouring positions
- dec_seg: int32 [2, 512], P('dp'), may hold values from 0 to 7, never falling along the last dimension, each value on 1 to 128 neighbouring positions
Outputs:
- context: bfloat16 [16, 2, 512, 4096], P('section', 'dp', None, 'mp')
- enc_grad: float32 [2, 512, 4096], P('dp', 'mp', 'section')
Inputs may be any that keep to these rules, and one draw needn't show every extreme that they name: `enc_seg`: document ids never fall along a sequence and every id appears. `dec_seg`: document ids never fall along a sequence and every id appears.
All inputs are finite; a program needn't handle non-finite values.
Results may differ from a plain program's by a relative error of at most 0.04.
The roundings to bfloat16 on the way count: a program that leaves them out, or rounds other values in their place, can miss the bound.
Values may be sent and summed in bfloat16 or wider, within the bound.
No kernel may reach another device: no remote copies, remote signals or barrier semaphores. Data moves between devices by JAX's collectives and lax.ppermute only.
A program may use at most 128 MiB of HBM per device.

v0:
```python
import functools

import jax
import jax.numpy as jnp
from jax import lax
from jax.experimental import pallas as pl
from jax.experimental.pallas import tpu as pltpu
from jax.sharding import Mesh, PartitionSpec as P

HD = 256
NZ, NC, NX, NY, ND = 8, 2, 4, 2, 2
TB = 64
FB = 256
NB = 8
VMEM = 24 << 20
AXES = ("z", "c", "x", "y")
NT = (((1,), (1,)), ((), ()))
TN = (((0,), (0,)), ((), ()))

Z_STEP = (0, 1, 2, 7)


def flat(z, c, x, y):
    return ((z * NC + c) * NX + x) * NY + y


SMALL_GROUPS = [[flat(z, 0, x, y) for z in range(NZ)] for x in range(NX) for y in range(NY)]
SMALL_GROUPS += [[flat(z, 1, x, y) for x in range(NX) for y in range(NY)] for z in range(NZ)]


def small_stage(value):
    return lax.all_to_all(value, AXES, 0, 0, axis_index_groups=SMALL_GROUPS)


def joint(value, move0, move1):
    pairs = []
    for z in range(NZ):
        for c in range(NC):
            for x in range(NX):
                for y in range(NY):
                    dz, dx, dy = (move0, move1)[c]
                    pairs.append((flat(z, c, x, y), flat((z + dz) % NZ, c, (x + dx) % NX, (y + dy) % NY)))
    return lax.ppermute(value, AXES, pairs)


def across(value):
    return joint(value, (0, 0, 1), (4, 0, 0))


def big_stage(value, i, sign):
    return joint(value, (0, sign * i, 0), (sign * Z_STEP[i], 0, 0))


def twin(value):
    return lax.ppermute(value, "c", [(0, 1), (1, 0)])


def whole(n):
    return [pl.BlockSpec(memory_space=pltpu.VMEM)] * n


HBM = pl.BlockSpec(memory_space=pltpu.HBM)
SMEM = pl.BlockSpec(memory_space=pltpu.SMEM)


def project_kernel(place_ref, *refs):
    own, other, w_ref = refs[:8], refs[8:16], refs[16]
    out_ref, w_buf, lhs_ref, acc_ref, sems = refs[17:]
    z, core, x, y = place_ref[0], place_ref[1], place_ref[2], place_ref[3]
    rows = 4 * FB

    def load(k):
        span = pl.ds(k * rows, rows)
        return pltpu.make_async_copy(w_ref.at[span, :], w_buf.at[span, :], sems.at[k])

    for k in range(4):
        load(k).start()

    def lay(even, odd):
        for b in range(2):
            for i in range(4):
                start = pl.multiple_of((((x + i) % NX) * NY + (y + b) % NY) * TB, TB)
                for k in range(NZ):
                    lhs_ref[2 * k, pl.ds(start, TB), :] = even[4 * b + i][k]
                lhs_ref[2 * ((z + Z_STEP[i] + 4 * b) % NZ) + 1] = odd[4 * b + i][...].reshape(NB * TB, FB)

    @pl.when(core == 0)
    def _():
        lay(own, other)

    @pl.when(core == 1)
    def _():
        lay(other, own)

    for k in range(4):
        load(k).wait()
        lhs = jnp.concatenate([lhs_ref[4 * k + n] for n in range(4)], axis=1)
        part = jnp.dot(lhs, w_buf[pl.ds(k * rows, rows), :], preferred_element_type=jnp.float32)
        if k == 0:
            acc_ref[...] = part
        elif k < 3:
            acc_ref[...] = acc_ref[...] + part
        else:
            out_ref[...] = (acc_ref[...] + part).astype(jnp.bfloat16)


def project(place, own, other, weight):
    depth, width = weight.shape
    rows = NB * TB
    return pl.pallas_call(
        project_kernel,
        in_specs=[SMEM] + whole(16) + [HBM],
        out_specs=whole(1)[0],
        scratch_shapes=[
            pltpu.VMEM((depth, width), jnp.bfloat16),
            pltpu.VMEM((2 * NZ, rows, FB), jnp.bfloat16),
            pltpu.VMEM((rows, width), jnp.float32),
            pltpu.SemaphoreType.DMA((4,)),
        ],
        out_shape=jax.ShapeDtypeStruct((rows, width), jnp.bfloat16),
        compiler_params=pltpu.CompilerParams(vmem_limit_bytes=VMEM),
        name="project",
    )(place, *own, *other, weight)


def attend_kernel(q_ref, g_ref, k_ref, v_ref, es_ref, ds_ref, ctx_ref, gk_ref, gv_ref):
    scale = HD ** -0.5
    q, g, k, v = q_ref[...], g_ref[...], k_ref[...], v_ref[...]
    same = es_ref[...] == ds_ref[...]
    scores = lax.dot_general(k, q, NT, preferred_element_type=jnp.float32) * scale
    scores = jnp.where(same, scores, -1e30)
    top = jnp.max(scores, axis=0, keepdims=True)
    raised = jnp.exp(scores - top)
    probs = raised / jnp.sum(raised, axis=0, keepdims=True)
    low = probs.astype(jnp.bfloat16)
    ctx_ref[...] = lax.dot_general(low, v, TN, preferred_element_type=jnp.float32).astype(jnp.bfloat16)
    gv_ref[...] = jnp.dot(low, g, preferred_element_type=jnp.float32).astype(jnp.bfloat16)
    gp = lax.dot_general(v, g, NT, preferred_element_type=jnp.float32)
    inner = jnp.sum(probs * gp, axis=0, keepdims=True)
    gs = (probs * (gp - inner) * scale).astype(jnp.bfloat16)
    gk_ref[...] = jnp.dot(gs, q, preferred_element_type=jnp.float32).astype(jnp.bfloat16)


def attend(query, grad, key_values, enc_col, dec_row):
    dec, width = query.shape
    enc = key_values.shape[0]
    heads = width // HD
    head = pl.BlockSpec((dec, HD), lambda h: (0, h))
    key = pl.BlockSpec((enc, HD), lambda h: (0, h))
    value = pl.BlockSpec((enc, HD), lambda h: (0, heads + h))
    return pl.pallas_call(
        attend_kernel,
        grid=(heads,),
        in_specs=[head, head, key, value, pl.BlockSpec((enc, 1), lambda h: (0, 0)), pl.BlockSpec((1, dec), lambda h: (0, 0))],
        out_specs=[head, key, key],
        out_shape=[
            jax.ShapeDtypeStruct((dec, width), jnp.bfloat16),
            jax.ShapeDtypeStruct((enc, width), jnp.bfloat16),
            jax.ShapeDtypeStruct((enc, width), jnp.bfloat16),
        ],
        compiler_params=pltpu.CompilerParams(vmem_limit_bytes=VMEM),
        name="attend",
    )(query, grad, key_values, key_values, enc_col, dec_row)


def spread_kernel(flip, place_ref, gk_ref, gv_ref, w_ref, out_ref, w_buf, sems):
    z, core, x, y = place_ref[0], place_ref[1], place_ref[2], place_ref[3]
    parity = 1 - core if flip else core
    width = gk_ref.shape[1]

    def load(k):
        start = pl.multiple_of(k * (2 * FB) + parity * FB, FB)
        return pltpu.make_async_copy(w_ref.at[pl.ds(start, FB), :], w_buf.at[k], sems.at[k])

    def place_out(k, out):
        @pl.when(parity == 0)
        def _():
            for m in range(NB):
                out_ref[(m + y) % NY, (m // NY + NX - x) % NX, k] = out[m]

        @pl.when(parity == 1)
        def _():
            away = (k + NZ - z) % NZ
            i = away % 4
            out_ref[(away // 4 + i // 3) % 2, i] = out

    for k in range(NZ):
        load(k).start()
    grads = jnp.concatenate([gk_ref[...], gv_ref[...]], axis=1)
    for k in range(0, NZ, 2):
        load(k).wait()
        load(k + 1).wait()
        rows = w_buf[pl.ds(k, 2)].reshape(2 * FB, 2 * width)
        out = lax.dot_general(grads, rows, NT, preferred_element_type=jnp.float32).astype(jnp.bfloat16)
        for n in range(2):
            place_out(k + n, out[:, n * FB:(n + 1) * FB].reshape(NB, TB, FB))


def spread(place, grad_keys, grad_values, weight, flip):
    return pl.pallas_call(
        functools.partial(spread_kernel, flip),
        in_specs=[SMEM] + whole(2) + [HBM],
        out_specs=whole(1)[0],
        scratch_shapes=[pltpu.VMEM((NZ, FB, weight.shape[1]), jnp.bfloat16), pltpu.SemaphoreType.DMA((NZ,))],
        out_shape=jax.ShapeDtypeStruct((2, 4, NB, TB, FB), jnp.bfloat16),
        compiler_params=pltpu.CompilerParams(vmem_limit_bytes=VMEM),
        name="spread_other" if flip else "spread_own",
    )(place, grad_keys, grad_values, weight)


def merge_kernel(one_ref, two_ref, *out_refs):
    for b in range(2):
        for i in range(4):
            both = one_ref[b, i].astype(jnp.float32) + two_ref[b, i].astype(jnp.float32)
            out_refs[4 * b + i][...] = both.astype(jnp.bfloat16)


def merge(one, two):
    shape = jax.ShapeDtypeStruct((NB, TB, FB), jnp.bfloat16)
    return pl.pallas_call(
        merge_kernel,
        in_specs=whole(2),
        out_specs=whole(8),
        out_shape=[shape] * 8,
        compiler_params=pltpu.CompilerParams(vmem_limit_bytes=VMEM),
        name="merge",
    )(one, two)


def total(parts):
    return functools.reduce(jnp.add, [p.astype(jnp.float32) for p in parts])


def per_device(enc_out, kv_weight, dec_query, ctx_grad, enc_seg, dec_seg):
    width = kv_weight.shape[3]
    place = jnp.stack([lax.axis_index(a) for a in AXES])

    near = small_stage(jnp.broadcast_to(enc_out, (NB, TB, FB)))
    far = across(near)
    own = [near] + [big_stage(near, i, -1) for i in (1, 2, 3)]
    far, *own, kv_weight = lax.optimization_barrier((far, *own, kv_weight))
    own += [far] + [big_stage(far, i, -1) for i in (1, 2, 3)]
    weight = kv_weight[0].reshape(kv_weight.shape[1], 2 * width)
    weight = pltpu.with_memory_space_constraint(weight, pltpu.HBM)
    *own[:5], weight = lax.optimization_barrier((*own[:5], weight))
    other = [twin(v) for v in own]
    key_values = project(place, own, other, weight)

    enc_col = enc_seg.reshape(NB * TB, 1)
    context, grad_keys, grad_values = attend(dec_query[0, 0], ctx_grad[0, 0], key_values, enc_col, dec_seg)

    theirs = twin(spread(place, grad_keys, grad_values, weight, True))
    mine = spread(place, grad_keys, grad_values, weight, False)
    parts = merge(mine, theirs)
    away = [parts[4]] + [big_stage(parts[4 + i], i, 1) for i in (1, 2, 3)]
    home = [parts[0]] + [big_stage(parts[i], i, 1) for i in (1, 2, 3)]
    crossed = across(total(away).astype(jnp.bfloat16))
    planes = total(home + [crossed]).astype(jnp.bfloat16)
    owned = jnp.sum(small_stage(planes).astype(jnp.float32), axis=0)
    return context[None, None], owned[None]


def solution(mesh):
    fine = Mesh(mesh.devices.reshape(NZ, NC, NX, NY, ND), ("z", "c", "x", "y", "d"))
    section, mp = ("z", "c"), ("x", "y")
    placed = (
        P("d", mp, section),
        P(section, None, None, mp),
        P(section, "d", None, mp),
        P(section, "d", None, mp),
        P("d", None),
        P("d", None),
    )
    return jax.shard_map(
        per_device,
        mesh=fine,
        in_specs=placed,
        out_specs=(P(section, "d", None, mp), P("d", mp, section)),
        check_vma=False,
    )
```

profile of v0, /device:TPU:1, one launch (start us, length us, event | category | flops | bytes accessed | tf_op | source)
XLA Modules:
  0.0 117.5 jit_solution(11130447055341981664)
XLA Ops:
  0.6 0.8 broadcast_in_dim.14
  1.4 14.6 %all_to_all.10.refs_0_ = bf16[8,64,256]{2,1,0:T(8,128)(2,1)S(1)} all-to-all(bf16[8,64,256]{2,1,0:T(8,128)(2,1)S(1)} %broadcast_in_dim.14), channel_id=1, replica_groups={{0,32,64,96,128,160,192,224},{2,34,66,98,130,162,194,226},{4,36,68,100,..., dimensions={0} | all-to-all | bytes 524288 | tf_op jit(solution)/shard_map/all_to_all | solution.py:32
  16.0 1.6 %collective-permute-start.3 = (bf16[8,64,256]{2,1,0:T(8,128)(2,1)S(1)}, bf16[8,64,256]{2,1,0:T(8,128)(2,1)S(1)}, u32[]{:S(2)}, u32[]{:S(2)}) collective-permute-start(bf16[8,64,256]{2,1,0:T(8,128)(2,1)S(1)} %all_to_all.10.refs_0_), channel_id=1, source_target_pairs={{0,4},{2,6},{4,8},{6,10},{8,12},{10,14},{12,0},{14,2},{16,48},{18,... | collective-permute-start | bytes 786440 | tf_op jit(solution)/shard_map/ppermute | solution.py:43
  17.6 5.1 %collective-permute-start.2 = (bf16[8,64,256]{2,1,0:T(8,128)(2,1)S(1)}, bf16[8,64,256]{2,1,0:T(8,128)(2,1)S(1)}, u32[]{:S(2)}, u32[]{:S(2)}) collective-permute-start(bf16[8,64,256]{2,1,0:T(8,128)(2,1)S(1)} %all_to_all.10.refs_0_), channel_id=1, source_target_pairs={{0,8},{2,10},{4,12},{6,14},{8,0},{10,2},{12,4},{14,6},{16,208},{18... | collective-permute-start | bytes 786440 | tf_op jit(solution)/shard_map/ppermute | solution.py:43
  23.5 2.1 %collective-permute-start = (bf16[8,64,256]{2,1,0:T(8,128)(2,1)S(1)}, bf16[8,64,256]{2,1,0:T(8,128)(2,1)S(1)}, u32[]{:S(2)}, u32[]{:S(2)}) collective-permute-start(bf16[8,64,256]{2,1,0:T(8,128)(2,1)S(1)} %all_to_all.10.refs_0_), channel_id=1, source_target_pairs={{0,2},{2,0},{4,6},{6,4},{8,10},{10,8},{12,14},{14,12},{16,144},{18... | collective-permute-start | bytes 786440 | tf_op jit(solution)/shard_map/ppermute | solution.py:43
  25.6 3.3 %collective-permute-done.2.refs_2_ = bf16[8,64,256]{2,1,0:T(8,128)(2,1)S(1)} collective-permute-done((bf16[8,64,256]{2,1,0:T(8,128)(2,1)S(1)}, bf16[8,64,256]{2,1,0:T(8,128)(2,1)S(1)}, u32[]{:S(2)}, u32[]{:S(2)}) %collective-permute-start.2) | collective-permute-done | bytes 262176 | tf_op jit(solution)/shard_map/ppermute | solution.py:43
  28.8 8.5 %collective-permute-done.1.refs_1_ = bf16[8,64,256]{2,1,0:T(8,128)(2,1)S(1)} collective-permute-done((bf16[8,64,256]{2,1,0:T(8,128)(2,1)S(1)}, bf16[8,64,256]{2,1,0:T(8,128)(2,1)S(1)}, u32[]{:S(2)}, u32[]{:S(2)}) %collective-permute-start.1) | collective-permute-done | bytes 262176 | tf_op jit(solution)/shard_map/ppermute | solution.py:43
  37.3 1.2 %collective-permute-start.6 = (bf16[8,64,256]{2,1,0:T(8,128)(2,1)S(1)}, bf16[8,64,256]{2,1,0:T(8,128)(2,1)S(1)}, u32[]{:S(2)}, u32[]{:S(2)}) collective-permute-start(bf16[8,64,256]{2,1,0:T(8,128)(2,1)S(1)} %collective-permute-done.refs_4_), channel_id=1, source_target_pairs={{0,4},{2,6},{4,8},{6,10},{8,12},{10,14},{12,0},{14,2},{16,48},{18,... | collective-permute-start | bytes 786440 | tf_op jit(solution)/shard_map/ppermute | solution.py:43
  38.5 3.4 %collective-permute-start.5 = (bf16[8,64,256]{2,1,0:T(8,128)(2,1)S(1)}, bf16[8,64,256]{2,1,0:T(8,128)(2,1)S(1)}, u32[]{:S(2)}, u32[]{:S(2)}) collective-permute-start(bf16[8,64,256]{2,1,0:T(8,128)(2,1)S(1)} %collective-permute-done.refs_4_), channel_id=1, source_target_pairs={{0,8},{2,10},{4,12},{6,14},{8,0},{10,2},{12,4},{14,6},{16,208},{18... | collective-permute-start | bytes 786440 | tf_op jit(solution)/shard_map/ppermute | solution.py:43
  41.9 9.4 %copy.9 = bf16[512,8,2,512]{3,1,2,0:T(8,128)(2,1)} copy(bf16[512,8,2,512]{3,2,1,0:T(2,128)(2,1)} %bitcast.18) | data formatting | bytes 16777216
  55.6 7.5 %project.1.k_ref.v_ref = bf16[512,1024]{1,0:T(8,128)(2,1)S(1)} custom-call(s32[4]{0:T(128)S(1)} %pad_add_fusion.place_ref, bf16[8,64,256]{2,1,0:T(8,128)(2,1)S(1)} %all_to_all.10.refs_0_, bf16[8,64,256]{2,1,0:T(8,128)(2,1)S(1)} %collective-permute-done.1.refs_1_, bf16[8,64,256]{2,1,0:T(8,128)(2,1)S(1)} %collective-permute-done.2.refs_2_, ...), custom_call_target="tpu_custom_call" | custom-call | tf_op jit(solution)/shard_map/project/pallas_call | solution.py:110
  63.1 3.9 %attend.1 = (bf16[512,512]{1,0:T(8,128)(2,1)}, bf16[512,512]{1,0:T(8,128)(2,1)S(1)}, bf16[512,512]{1,0:T(8,128)(2,1)S(1)}) custom-call(bf16[512,512]{1,0:T(8,128)(2,1)S(1)} %bitcast.13, bf16[512,512]{1,0:T(8,128)(2,1)S(1)} %bitcast.14, bf16[512,1024]{1,0:T(8,128)(2,1)S(1)} %project.1.k_ref.v_ref, bf16[512,1024]{1,0:T(8,128)(2,1)S(1)} %project.1.k_ref.v_ref, ...), custom_call_target="tpu_custom_call" | custom-call | tf_op jit(solution)/shard_map/attend/pallas_call | solution.py:151
  67.1 5.1 %spread_other.1 = bf16[2,4,8,64,256]{4,3,2,1,0:T(8,128)(2,1)S(1)} custom-call(s32[4]{0:T(128)S(1)} %pad_add_fusion.place_ref, bf16[512,512]{1,0:T(8,128)(2,1)S(1)} %get-tuple-element.38.gk_ref, bf16[512,512]{1,0:T(8,128)(2,1)S(1)} %get-tuple-element.39.gv_ref, bf16[4096,1024]{1,0:T(8,128)(2,1)} %bitcast.16), custom_call_target="tpu_custom_call" | custom-call | tf_op jit(solution)/shard_map/spread_other/pallas_call | solution.py:200
  72.5 5.1 %spread_own.1.one_ref = bf16[2,4,8,64,256]{4,3,2,1,0:T(8,128)(2,1)S(1)} custom-call(s32[4]{0:T(128)S(1)} %pad_add_fusion.place_ref, bf16[512,512]{1,0:T(8,128)(2,1)S(1)} %get-tuple-element.38.gk_ref, bf16[512,512]{1,0:T(8,128)(2,1)S(1)} %get-tuple-element.39.gv_ref, bf16[4096,1024]{1,0:T(8,128)(2,1)} %bitcast.17), custom_call_target="tpu_custom_call" | custom-call | tf_op jit(solution)/shard_map/spread_own/pallas_call | solution.py:200
  78.1 1.7 %collective-permute-start.19 = (bf16[8,64,256]{2,1,0:T(8,128)(2,1)S(1)}, bf16[8,64,256]{2,1,0:T(8,128)(2,1)S(1)}, u32[]{:S(2)}, u32[]{:S(2)}) collective-permute-start(bf16[8,64,256]{2,1,0:T(8,128)(2,1)S(1)} %get-tuple-element.45), channel_id=1, source_target_pairs={{0,4},{2,6},{4,8},{6,10},{8,12},{10,14},{12,0},{14,2},{16,48},{18,... | collective-permute-start | bytes 786440 | tf_op jit(solution)/shard_map/ppermute | solution.py:43
  80.3 2.0 %collective-permute-start.21 = (bf16[8,64,256]{2,1,0:T(8,128)(2,1)S(1)}, bf16[8,64,256]{2,1,0:T(8,128)(2,1)S(1)}, u32[]{:S(2)}, u32[]{:S(2)}) collective-permute-start(bf16[8,64,256]{2,1,0:T(8,128)(2,1)S(1)} %get-tuple-element.47), channel_id=1, source_target_pairs={{0,12},{2,14},{4,0},{6,2},{8,4},{10,6},{12,8},{14,10},{16,240},{18... | collective-permute-start | bytes 786440 | tf_op jit(solution)/shard_map/ppermute | solution.py:43
  82.3 2.4 %collective-permute-start.17 = (bf16[8,64,256]{2,1,0:T(8,128)(2,1)S(1)}, bf16[8,64,256]{2,1,0:T(8,128)(2,1)S(1)}, u32[]{:S(2)}, u32[]{:S(2)}) collective-permute-start(bf16[8,64,256]{2,1,0:T(8,128)(2,1)S(1)} %get-tuple-element.42), channel_id=1, source_target_pairs={{0,8},{2,10},{4,12},{6,14},{8,0},{10,2},{12,4},{14,6},{16,80},{18,... | collective-permute-start | bytes 786440 | tf_op jit(solution)/shard_map/ppermute | solution.py:43
  84.7 1.6 %collective-permute-done.19 = bf16[8,64,256]{2,1,0:T(8,128)(2,1)S(1)} collective-permute-done((bf16[8,64,256]{2,1,0:T(8,128)(2,1)S(1)}, bf16[8,64,256]{2,1,0:T(8,128)(2,1)S(1)}, u32[]{:S(2)}, u32[]{:S(2)}) %collective-permute-start.19) | collective-permute-done | bytes 262176 | tf_op jit(solution)/shard_map/ppermute | solution.py:43
  86.4 3.0 %collective-permute-done.20 = bf16[8,64,256]{2,1,0:T(8,128)(2,1)S(1)} collective-permute-done((bf16[8,64,256]{2,1,0:T(8,128)(2,1)S(1)}, bf16[8,64,256]{2,1,0:T(8,128)(2,1)S(1)}, u32[]{:S(2)}, u32[]{:S(2)}) %collective-permute-start.20) | collective-permute-done | bytes 262176 | tf_op jit(solution)/shard_map/ppermute | solution.py:43
  89.6 3.2 %collective-permute-start.22 = (bf16[8,64,256]{2,1,0:T(8,128)(2,1)S(1)}, bf16[8,64,256]{2,1,0:T(8,128)(2,1)S(1)}, u32[]{:S(2)}, u32[]{:S(2)}) collective-permute-start(bf16[8,64,256]{2,1,0:T(8,128)(2,1)S(1)} %add_convert_fusion.1), channel_id=1, source_target_pairs={{0,2},{2,0},{4,6},{6,4},{8,10},{10,8},{12,14},{14,12},{16,144},{18... | collective-permute-start | bytes 786440 | tf_op jit(solution)/shard_map/ppermute | solution.py:43
  92.8 1.7 %collective-permute-done.16 = bf16[8,64,256]{2,1,0:T(8,128)(2,1)S(1)} collective-permute-done((bf16[8,64,256]{2,1,0:T(8,128)(2,1)S(1)}, bf16[8,64,256]{2,1,0:T(8,128)(2,1)S(1)}, u32[]{:S(2)}, u32[]{:S(2)}) %collective-permute-start.16) | collective-permute-done | bytes 262176 | tf_op jit(solution)/shard_map/ppermute | solution.py:43
  94.4 3.6 %collective-permute-done.17 = bf16[8,64,256]{2,1,0:T(8,128)(2,1)S(1)} collective-permute-done((bf16[8,64,256]{2,1,0:T(8,128)(2,1)S(1)}, bf16[8,64,256]{2,1,0:T(8,128)(2,1)S(1)}, u32[]{:S(2)}, u32[]{:S(2)}) %collective-permute-start.17) | collective-permute-done | bytes 262176 | tf_op jit(solution)/shard_map/ppermute | solution.py:43
  98.0 8.5 %collective-permute-done.22 = bf16[8,64,256]{2,1,0:T(8,128)(2,1)S(1)} collective-permute-done((bf16[8,64,256]{2,1,0:T(8,128)(2,1)S(1)}, bf16[8,64,256]{2,1,0:T(8,128)(2,1)S(1)}, u32[]{:S(2)}, u32[]{:S(2)}) %collective-permute-start.22) | collective-permute-done | bytes 262176 | tf_op jit(solution)/shard_map/ppermute | solution.py:43
  106.7 10.2 %all_to_all.11 = bf16[8,64,256]{2,1,0:T(8,128)(2,1)S(1)} all-to-all(bf16[8,64,256]{2,1,0:T(8,128)(2,1)S(1)} %add_convert_fusion), channel_id=1, replica_groups={{0,32,64,96,128,160,192,224},{2,34,66,98,130,162,194,226},{4,36,68,100,..., dimensions={0} | all-to-all | bytes 524288 | tf_op jit(solution)/shard_map/all_to_all | solution.py:32
  (44 shorter events, 7.2 us)
Async XLA Ops:
  16.0 9.6 %collective-permute-start.3 = (bf16[8,64,256]{2,1,0:T(8,128)(2,1)S(1)}, bf16[8,64,256]{2,1,0:T(8,128)(2,1)S(1)}, u32[]{:S(2)}, u32[]{:S(2)}) collective-permute-start(bf16[8,64,256]{2,1,0:T(8,128)(2,1)S(1)} %all_to_all.10.refs_0_), channel_id=1, source_target_pairs={{0,4},{2,6},{4,8},{6,10},{8,12},{10,14},{12,0},{14,2},{16,48},{18,... | collective-permute-start | bytes 786440 | tf_op jit(solution)/shard_map/ppermute | solution.py:43
  17.6 11.2 %collective-permute-start.2 = (bf16[8,64,256]{2,1,0:T(8,128)(2,1)S(1)}, bf16[8,64,256]{2,1,0:T(8,128)(2,1)S(1)}, u32[]{:S(2)}, u32[]{:S(2)}) collective-permute-start(bf16[8,64,256]{2,1,0:T(8,128)(2,1)S(1)} %all_to_all.10.refs_0_), channel_id=1, source_target_pairs={{0,8},{2,10},{4,12},{6,14},{8,0},{10,2},{12,4},{14,6},{16,208},{18... | collective-permute-start | bytes 786440 | tf_op jit(solution)/shard_map/ppermute | solution.py:43
  22.7 14.6 %collective-permute-start.1 = (bf16[8,64,256]{2,1,0:T(8,128)(2,1)S(1)}, bf16[8,64,256]{2,1,0:T(8,128)(2,1)S(1)}, u32[]{:S(2)}, u32[]{:S(2)}) collective-permute-start(bf16[8,64,256]{2,1,0:T(8,128)(2,1)S(1)} %all_to_all.10.refs_0_), channel_id=1, source_target_pairs={{0,12},{2,14},{4,0},{6,2},{8,4},{10,6},{12,8},{14,10},{16,240},{18... | collective-permute-start | bytes 786440 | tf_op jit(solution)/shard_map/ppermute | solution.py:43
  23.5 13.8 %collective-permute-start = (bf16[8,64,256]{2,1,0:T(8,128)(2,1)S(1)}, bf16[8,64,256]{2,1,0:T(8,128)(2,1)S(1)}, u32[]{:S(2)}, u32[]{:S(2)}) collective-permute-start(bf16[8,64,256]{2,1,0:T(8,128)(2,1)S(1)} %all_to_all.10.refs_0_), channel_id=1, source_target_pairs={{0,2},{2,0},{4,6},{6,4},{8,10},{10,8},{12,14},{14,12},{16,144},{18... | collective-permute-start | bytes 786440 | tf_op jit(solution)/shard_map/ppermute | solution.py:43
  37.3 14.5 %collective-permute-start.6 = (bf16[8,64,256]{2,1,0:T(8,128)(2,1)S(1)}, bf16[8,64,256]{2,1,0:T(8,128)(2,1)S(1)}, u32[]{:S(2)}, u32[]{:S(2)}) collective-permute-start(bf16[8,64,256]{2,1,0:T(8,128)(2,1)S(1)} %collective-permute-done.refs_4_), channel_id=1, source_target_pairs={{0,4},{2,6},{4,8},{6,10},{8,12},{10,14},{12,0},{14,2},{16,48},{18,... | collective-permute-start | bytes 786440 | tf_op jit(solution)/shard_map/ppermute | solution.py:43
  38.5 13.3 %collective-permute-start.5 = (bf16[8,64,256]{2,1,0:T(8,128)(2,1)S(1)}, bf16[8,64,256]{2,1,0:T(8,128)(2,1)S(1)}, u32[]{:S(2)}, u32[]{:S(2)}) collective-permute-start(bf16[8,64,256]{2,1,0:T(8,128)(2,1)S(1)} %collective-permute-done.refs_4_), channel_id=1, source_target_pairs={{0,8},{2,10},{4,12},{6,14},{8,0},{10,2},{12,4},{14,6},{16,208},{18... | collective-permute-start | bytes 786440 | tf_op jit(solution)/shard_map/ppermute | solution.py:43
  41.9 10.4 %collective-permute-start.4 = (bf16[8,64,256]{2,1,0:T(8,128)(2,1)S(1)}, bf16[8,64,256]{2,1,0:T(8,128)(2,1)S(1)}, u32[]{:S(2)}, u32[]{:S(2)}) collective-permute-start(bf16[8,64,256]{2,1,0:T(8,128)(2,1)S(1)} %collective-permute-done.refs_4_), channel_id=1, source_target_pairs={{0,12},{2,14},{4,0},{6,2},{8,4},{10,6},{12,8},{14,10},{16,240},{18... | collective-permute-start | bytes 786440 | tf_op jit(solution)/shard_map/ppermute | solution.py:43
  41.9 11.8 %copy-start.3 = (s32[1,512]{1,0:T(1,128)S(1)}, s32[1,512]{1,0:T(1,128)}, u32[]{:S(2)}) copy-start(s32[1,512]{1,0:T(1,128)} %param.10) | copy-start | bytes 6148
  51.3 1.5 %collective-permute-start.7 = (bf16[8,64,256]{2,1,0:T(8,128)(2,1)S(1)}, bf16[8,64,256]{2,1,0:T(8,128)(2,1)S(1)}, u32[]{:S(2)}, u32[]{:S(2)}) collective-permute-start(bf16[8,64,256]{2,1,0:T(8,128)(2,1)S(1)} %all_to_all.10.refs_0_), channel_id=1, source_target_pairs={{0,16},{16,0},{1,17},{17,1},{2,18},{18,2},{3,19},{19,3},{4,20},{20... | collective-permute-start | bytes 786440 | tf_op jit(solution)/shard_map/ppermute | solution.py:55
  51.3 1.9 %collective-permute-start.8 = (bf16[8,64,256]{2,1,0:T(8,128)(2,1)S(1)}, bf16[8,64,256]{2,1,0:T(8,128)(2,1)S(1)}, u32[]{:S(2)}, u32[]{:S(2)}) collective-permute-start(bf16[8,64,256]{2,1,0:T(8,128)(2,1)S(1)} %collective-permute-done.1.refs_1_), channel_id=1, source_target_pairs={{0,16},{16,0},{1,17},{17,1},{2,18},{18,2},{3,19},{19,3},{4,20},{20... | collective-permute-start | bytes 786440 | tf_op jit(solution)/shard_map/ppermute | solution.py:55
  51.8 1.8 %collective-permute-start.9 = (bf16[8,64,256]{2,1,0:T(8,128)(2,1)S(1)}, bf16[8,64,256]{2,1,0:T(8,128)(2,1)S(1)}, u32[]{:S(2)}, u32[]{:S(2)}) collective-permute-start(bf16[8,64,256]{2,1,0:T(8,128)(2,1)S(1)} %collective-permute-done.2.refs_2_), channel_id=1, source_target_pairs={{0,16},{16,0},{1,17},{17,1},{2,18},{18,2},{3,19},{19,3},{4,20},{20... | collective-permute-start | bytes 786440 | tf_op jit(solution)/shard_map/ppermute | solution.py:55
  51.8 2.5 %collective-permute-start.10 = (bf16[8,64,256]{2,1,0:T(8,128)(2,1)S(1)}, bf16[8,64,256]{2,1,0:T(8,128)(2,1)S(1)}, u32[]{:S(2)}, u32[]{:S(2)}) collective-permute-start(bf16[8,64,256]{2,1,0:T(8,128)(2,1)S(1)} %collective-permute-done.3.refs_3_), channel_id=1, source_target_pairs={{0,16},{16,0},{1,17},{17,1},{2,18},{18,2},{3,19},{19,3},{4,20},{20... | collective-permute-start | bytes 786440 | tf_op jit(solution)/shard_map/ppermute | solution.py:55
  52.3 2.1 %collective-permute-start.11 = (bf16[8,64,256]{2,1,0:T(8,128)(2,1)S(1)}, bf16[8,64,256]{2,1,0:T(8,128)(2,1)}, u32[]{:S(2)}, u32[]{:S(2)}) collective-permute-start(bf16[8,64,256]{2,1,0:T(8,128)(2,1)S(1)} %collective-permute-done.refs_4_), channel_id=1, source_target_pairs={{0,16},{16,0},{1,17},{17,1},{2,18},{18,2},{3,19},{19,3},{4,20},{20... | collective-permute-start | bytes 786440 | tf_op jit(solution)/shard_map/ppermute | solution.py:55
  52.8 2.0 %collective-permute-start.14 = (bf16[8,64,256]{2,1,0:T(8,128)(2,1)S(1)}, bf16[8,64,256]{2,1,0:T(8,128)(2,1)}, u32[]{:S(2)}, u32[]{:S(2)}) collective-permute-start(bf16[8,64,256]{2,1,0:T(8,128)(2,1)S(1)} %collective-permute-done.6.refs_7_), channel_id=1, source_target_pairs={{0,16},{16,0},{1,17},{17,1},{2,18},{18,2},{3,19},{19,3},{4,20},{20... | collective-permute-start | bytes 786440 | tf_op jit(solution)/shard_map/ppermute | solution.py:55
  53.2 2.0 %collective-permute-start.13 = (bf16[8,64,256]{2,1,0:T(8,128)(2,1)S(1)}, bf16[8,64,256]{2,1,0:T(8,128)(2,1)}, u32[]{:S(2)}, u32[]{:S(2)}) collective-permute-start(bf16[8,64,256]{2,1,0:T(8,128)(2,1)S(1)} %collective-permute-done.5.refs_6_), channel_id=1, source_target_pairs={{0,16},{16,0},{1,17},{17,1},{2,18},{18,2},{3,19},{19,3},{4,20},{20... | collective-permute-start | bytes 786440 | tf_op jit(solution)/shard_map/ppermute | solution.py:55
  53.6 2.0 %collective-permute-start.12 = (bf16[8,64,256]{2,1,0:T(8,128)(2,1)S(1)}, bf16[8,64,256]{2,1,0:T(8,128)(2,1)}, u32[]{:S(2)}, u32[]{:S(2)}) collective-permute-start(bf16[8,64,256]{2,1,0:T(8,128)(2,1)S(1)} %collective-permute-done.4.refs_5_), channel_id=1, source_target_pairs={{0,16},{16,0},{1,17},{17,1},{2,18},{18,2},{3,19},{19,3},{4,20},{20... | collective-permute-start | bytes 786440 | tf_op jit(solution)/shard_map/ppermute | solution.py:55
  72.2 5.4 %collective-permute-start.15 = (bf16[2,4,8,64,256]{4,3,2,1,0:T(8,128)(2,1)S(1)}, bf16[2,4,8,64,256]{4,3,2,1,0:T(8,128)(2,1)S(1)}, u32[]{:S(2)}, u32[]{:S(2)}) collective-permute-start(bf16[2,4,8,64,256]{4,3,2,1,0:T(8,128)(2,1)S(1)} %spread_other.1), channel_id=1, source_target_pairs={{0,16},{16,0},{1,17},{17,1},{2,18},{18,2},{3,19},{19,3},{4,20},{20... | collective-permute-start | bytes 6291464 | tf_op jit(solution)/shard_map/ppermute | solution.py:55
  78.1 8.3 %collective-permute-start.19 = (bf16[8,64,256]{2,1,0:T(8,128)(2,1)S(1)}, bf16[8,64,256]{2,1,0:T(8,128)(2,1)S(1)}, u32[]{:S(2)}, u32[]{:S(2)}) collective-permute-start(bf16[8,64,256]{2,1,0:T(8,128)(2,1)S(1)} %get-tuple-element.45), channel_id=1, source_target_pairs={{0,4},{2,6},{4,8},{6,10},{8,12},{10,14},{12,0},{14,2},{16,48},{18,... | collective-permute-start | bytes 786440 | tf_op jit(solution)/shard_map/ppermute | solution.py:43
  79.8 9.6 %collective-permute-start.20 = (bf16[8,64,256]{2,1,0:T(8,128)(2,1)S(1)}, bf16[8,64,256]{2,1,0:T(8,128)(2,1)S(1)}, u32[]{:S(2)}, u32[]{:S(2)}) collective-permute-start(bf16[8,64,256]{2,1,0:T(8,128)(2,1)S(1)} %get-tuple-element.46), channel_id=1, source_target_pairs={{0,8},{2,10},{4,12},{6,14},{8,0},{10,2},{12,4},{14,6},{16,80},{18,... | collective-permute-start | bytes 786440 | tf_op jit(solution)/shard_map/ppermute | solution.py:43
  80.3 9.1 %collective-permute-start.21 = (bf16[8,64,256]{2,1,0:T(8,128)(2,1)S(1)}, bf16[8,64,256]{2,1,0:T(8,128)(2,1)S(1)}, u32[]{:S(2)}, u32[]{:S(2)}) collective-permute-start(bf16[8,64,256]{2,1,0:T(8,128)(2,1)S(1)} %get-tuple-element.47), channel_id=1, source_target_pairs={{0,12},{2,14},{4,0},{6,2},{8,4},{10,6},{12,8},{14,10},{16,240},{18... | collective-permute-start | bytes 786440 | tf_op jit(solution)/shard_map/ppermute | solution.py:43
  82.3 12.1 %collective-permute-start.16 = (bf16[8,64,256]{2,1,0:T(8,128)(2,1)S(1)}, bf16[8,64,256]{2,1,0:T(8,128)(2,1)S(1)}, u32[]{:S(2)}, u32[]{:S(2)}) collective-permute-start(bf16[8,64,256]{2,1,0:T(8,128)(2,1)S(1)} %get-tuple-element.41), channel_id=1, source_target_pairs={{0,4},{2,6},{4,8},{6,10},{8,12},{10,14},{12,0},{14,2},{16,48},{18,... | collective-permute-start | bytes 786440 | tf_op jit(solution)/shard_map/ppermute | solution.py:43
  82.3 15.7 %collective-permute-start.17 = (bf16[8,64,256]{2,1,0:T(8,128)(2,1)S(1)}, bf16[8,64,256]{2,1,0:T(8,128)(2,1)S(1)}, u32[]{:S(2)}, u32[]{:S(2)}) collective-permute-start(bf16[8,64,256]{2,1,0:T(8,128)(2,1)S(1)} %get-tuple-element.42), channel_id=1, source_target_pairs={{0,8},{2,10},{4,12},{6,14},{8,0},{10,2},{12,4},{14,6},{16,80},{18,... | collective-permute-start | bytes 786440 | tf_op jit(solution)/shard_map/ppermute | solution.py:43
  86.4 11.7 %collective-permute-start.18 = (bf16[8,64,256]{2,1,0:T(8,128)(2,1)S(1)}, bf16[8,64,256]{2,1,0:T(8,128)(2,1)S(1)}, u32[]{:S(2)}, u32[]{:S(2)}) collective-permute-start(bf16[8,64,256]{2,1,0:T(8,128)(2,1)S(1)} %get-tuple-element.43), channel_id=1, source_target_pairs={{0,12},{2,14},{4,0},{6,2},{8,4},{10,6},{12,8},{14,10},{16,240},{18... | collective-permute-start | bytes 786440 | tf_op jit(solution)/shard_map/ppermute | solution.py:43
  89.6 16.9 %collective-permute-start.22 = (bf16[8,64,256]{2,1,0:T(8,128)(2,1)S(1)}, bf16[8,64,256]{2,1,0:T(8,128)(2,1)S(1)}, u32[]{:S(2)}, u32[]{:S(2)}) collective-permute-start(bf16[8,64,256]{2,1,0:T(8,128)(2,1)S(1)} %add_convert_fusion.1), channel_id=1, source_target_pairs={{0,2},{2,0},{4,6},{6,4},{8,10},{10,8},{12,14},{14,12},{16,144},{18... | collective-permute-start | bytes 786440 | tf_op jit(solution)/shard_map/ppermute | solution.py:43
  (3 other events, 27.4 us)
where the time goes:
time: 118 us
  waiting for transfers between devices  32.7 us (28%)
  starting transfers between devices  25.8 us (22%)
  blocking collectives  24.7 us (21%)
  Pallas kernels  22.2 us (19%)
  local copies, waits for them, and re-layouts  10.3 us (9%)
    ppermute x14, waiting for transfers between devices, joint(): return lax.ppermute(value, AXES, pairs)  30.2 us
    all_to_all x2, blocking collectives, small_stage(): return lax.all_to_all(value, AXES, 0, 0, axis_index_groups=SMALL_GROUPS)  24.7 us
    ppermute x14, starting transfers between devices, joint(): return lax.ppermute(value, AXES, pairs)  24 us
    pallas_call x2, Pallas kernels, spread(): pl.pallas_call(functools.partial(spread_kernel, flip), in_specs=[SMEM] +...  10.3 us
    unnamed x9, local copies, waits for them, and re-layouts  9.42 us
    pallas_call x1, Pallas kernels, project(): pl.pallas_call(project_kernel, in_specs=[SMEM] + whole(16) + [HBM], out_s...  7.48 us
    pallas_call x1, Pallas kernels, attend(): pl.pallas_call(attend_kernel, grid=(heads,), in_specs=[head, head, key, v...  3.94 us
    ppermute x9, waiting for transfers between devices, twin(): return lax.ppermute(value, 'c', [(0, 1), (1, 0)])  2.51 us
  transfers between devices with their start and end apart: 23, of which 15 were waited for; matrix products, arithmetic and copies ran while one was open for 8% of the time, Pallas kernels for 4%

commit v1 on v0

v1 whole, which is shorter than its diff:
```python
import functools

import jax
import jax.numpy as jnp
from jax import lax
from jax.experimental import pallas as pl
from jax.experimental.pallas import tpu as pltpu
from jax.sharding import Mesh, PartitionSpec as P

HD = 256
NZ, NC, NX, NY, ND = 8, 2, 4, 2, 2
TB = 64
FB = 256
NB = 8
VMEM = 20 << 20
AXES = ("z", "c", "x", "y")
NT = (((1,), (1,)), ((), ()))
TN = (((0,), (0,)), ((), ()))

Z_STEP = (0, 1, 2, 7)


def flat(z, c, x, y):
    return ((z * NC + c) * NX + x) * NY + y


SMALL_GROUPS = [[flat(z, 0, x, y) for z in range(NZ)] for x in range(NX) for y in range(NY)]
SMALL_GROUPS += [[flat(z, 1, x, y) for x in range(NX) for y in range(NY)] for z in range(NZ)]


def small_stage(value):
    return lax.all_to_all(value, AXES, 0, 0, axis_index_groups=SMALL_GROUPS)


def joint(value, move0, move1):
    pairs = []
    for z in range(NZ):
        for c in range(NC):
            for x in range(NX):
                for y in range(NY):
                    dz, dx, dy = (move0, move1)[c]
                    pairs.append((flat(z, c, x, y), flat((z + dz) % NZ, c, (x + dx) % NX, (y + dy) % NY)))
    return lax.ppermute(value, AXES, pairs)


def across(value):
    return joint(value, (0, 0, 1), (4, 0, 0))


def big_stage(value, i, sign):
    return joint(value, (0, sign * i, 0), (sign * Z_STEP[i], 0, 0))


def twin(value):
    return lax.ppermute(value, "c", [(0, 1), (1, 0)])


def whole(n):
    return [pl.BlockSpec(memory_space=pltpu.VMEM)] * n


HBM = pl.BlockSpec(memory_space=pltpu.HBM)
SMEM = pl.BlockSpec(memory_space=pltpu.SMEM)


def relayout_kernel(w_ref, out_ref, mark_ref, raw_ref, done_ref, load_sems, store_sems):
    def load(k):
        return pltpu.make_async_copy(w_ref.at[0, pl.ds(k * NC * FB, NC * FB)], raw_ref.at[k], load_sems.at[k])

    def store(k):
        return pltpu.make_async_copy(done_ref.at[k], out_ref.at[k], store_sems.at[k])

    for k in range(NZ):
        load(k).start()
    mark_ref[...] = jnp.zeros(mark_ref.shape, mark_ref.dtype)
    for k in range(NZ):
        load(k).wait()
        done_ref[k] = raw_ref[k].reshape(done_ref.shape[1:])
        store(k).start()
    for k in range(NZ):
        store(k).wait()


def relayout(weight):
    width = weight.shape[3]
    shape = (NZ, NC, FB, 2 * width)
    return pl.pallas_call(
        relayout_kernel,
        in_specs=[HBM],
        out_specs=[HBM] + whole(1),
        scratch_shapes=[
            pltpu.VMEM((NZ, NC * FB, 2, width), jnp.bfloat16),
            pltpu.VMEM(shape, jnp.bfloat16),
            pltpu.SemaphoreType.DMA((NZ,)),
            pltpu.SemaphoreType.DMA((NZ,)),
        ],
        out_shape=[pltpu.HBM(shape, jnp.bfloat16), jax.ShapeDtypeStruct((8, 128), jnp.float32)],
        compiler_params=pltpu.CompilerParams(vmem_limit_bytes=20 << 20),
        name="relayout",
    )(weight)


def lay_out(out_ref, parity, z, x, y, k, out):
    @pl.when(parity == 0)
    def _():
        for m in range(NB):
            out_ref[(m + y) % NY, (m // NY + NX - x) % NX, k] = out[m]

    @pl.when(parity == 1)
    def _():
        away = (k + NZ - z) % NZ
        i = away % 4
        out_ref[(away // 4 + i // 3) % 2, i] = out


def load_weights(w_ref, w_buf, sems, k, core, slot):
    return pltpu.make_async_copy(w_ref.at[k, core], w_buf.at[k, slot], sems.at[k, slot])


def spread(grads, w_buf, slot, out_ref, parity, z, x, y, ready):
    for k in range(0, NZ, 2):
        ready(k)
        ready(k + 1)
        rows = w_buf[pl.ds(k, 2), slot].reshape(2 * FB, grads.shape[1])
        out = lax.dot_general(grads, rows, NT, preferred_element_type=jnp.float32).astype(jnp.bfloat16)
        for n in range(2):
            lay_out(out_ref, parity, z, x, y, k + n, out[:, n * FB:(n + 1) * FB].reshape(NB, TB, FB))


def attend(q, g, k, v, same):
    scale = HD ** -0.5
    scores = lax.dot_general(k, q, NT, preferred_element_type=jnp.float32) * scale
    scores = jnp.where(same, scores, -1e30)
    top = jnp.max(scores, axis=0, keepdims=True)
    raised = jnp.exp(scores - top)
    probs = raised / jnp.sum(raised, axis=0, keepdims=True)
    low = probs.astype(jnp.bfloat16)
    context = lax.dot_general(low, v, TN, preferred_element_type=jnp.float32).astype(jnp.bfloat16)
    grad_values = jnp.dot(low, g, preferred_element_type=jnp.float32).astype(jnp.bfloat16)
    gp = lax.dot_general(v, g, NT, preferred_element_type=jnp.float32)
    inner = jnp.sum(probs * gp, axis=0, keepdims=True)
    gs = (probs * (gp - inner) * scale).astype(jnp.bfloat16)
    grad_keys = jnp.dot(gs, q, preferred_element_type=jnp.float32).astype(jnp.bfloat16)
    return context, grad_keys, grad_values


def main_kernel(place_ref, *refs):
    own, other = refs[:8], refs[8:16]
    w_ref, _, q_ref, g_ref, es_ref, ds_ref, ctx_ref, grad_ref, out_ref, w_buf, lhs_ref, acc_ref, kv_ref, sems = refs[16:]
    z, core, x, y = place_ref[0], place_ref[1], place_ref[2], place_ref[3]
    dec, width = q_ref.shape
    enc = NB * TB

    for k in range(NZ):
        for c in range(NC):
            load_weights(w_ref, w_buf, sems, k, c, c).start()

    def lay(even, odd):
        for b in range(2):
            for i in range(4):
                start = pl.multiple_of((((x + i) % NX) * NY + (y + b) % NY) * TB, TB)
                for k in range(NZ):
                    lhs_ref[2 * k, pl.ds(start, TB), :] = even[4 * b + i][k]
                lhs_ref[2 * ((z + Z_STEP[i] + 4 * b) % NZ) + 1] = odd[4 * b + i][...].reshape(enc, FB)

    @pl.when(core == 0)
    def _():
        lay(own, other)

    @pl.when(core == 1)
    def _():
        lay(other, own)

    for k in range(0, NZ, 2):
        for n in range(4):
            load_weights(w_ref, w_buf, sems, k + n // 2, n % 2, n % 2).wait()
        lhs = jnp.concatenate([lhs_ref[2 * k + n] for n in range(4)], axis=1)
        rows = w_buf[pl.ds(k, 2)].reshape(4 * FB, 2 * width)
        part = jnp.dot(lhs, rows, preferred_element_type=jnp.float32)
        if k == 0:
            acc_ref[...] = part
        elif k < NZ - 2:
            acc_ref[...] = acc_ref[...] + part
        else:
            kv_ref[...] = (acc_ref[...] + part).astype(jnp.bfloat16)

    same = es_ref[...] == ds_ref[...]
    for h in range(width // HD):
        head = pl.ds(h * HD, HD)
        value = pl.ds(width + h * HD, HD)
        found = attend(q_ref[:, head], g_ref[:, head], kv_ref[:, head], kv_ref[:, value], same)
        ctx_ref[:, head], grad_ref[:, head], grad_ref[:, value] = found

    spread(grad_ref[...], w_buf, 1 - core, out_ref, 1 - core, z, x, y, lambda k: None)


def main(place, own, other, weight, mark, query, grad, enc_col, dec_row):
    dec, width = query.shape
    enc = NB * TB
    return pl.pallas_call(
        main_kernel,
        in_specs=[SMEM] + whole(16) + [HBM] + whole(5),
        out_specs=whole(3),
        scratch_shapes=[
            pltpu.VMEM((NZ, NC, FB, 2 * width), jnp.bfloat16),
            pltpu.VMEM((2 * NZ, enc, FB), jnp.bfloat16),
            pltpu.VMEM((enc, 2 * width), jnp.float32),
            pltpu.VMEM((enc, 2 * width), jnp.bfloat16),
            pltpu.SemaphoreType.DMA((NZ, NC)),
        ],
        out_shape=[
            jax.ShapeDtypeStruct((dec, width), jnp.bfloat16),
            jax.ShapeDtypeStruct((enc, 2 * width), jnp.bfloat16),
            jax.ShapeDtypeStruct((2, 4, NB, TB, FB), jnp.bfloat16),
        ],
        compiler_params=pltpu.CompilerParams(vmem_limit_bytes=28 << 20),
        name="main",
    )(place, *own, *other, weight, mark, query, grad, enc_col, dec_row)


def own_kernel(place_ref, grad_ref, w_ref, out_ref, w_buf, sems):
    z, core, x, y = place_ref[0], place_ref[1], place_ref[2], place_ref[3]
    for k in range(NZ):
        load_weights(w_ref, w_buf, sems, k, core, 0).start()
    ready = lambda k: load_weights(w_ref, w_buf, sems, k, core, 0).wait()
    spread(grad_ref[...], w_buf, 0, out_ref, core, z, x, y, ready)


def spread_own(place, grads, weight):
    return pl.pallas_call(
        own_kernel,
        in_specs=[SMEM] + whole(1) + [HBM],
        out_specs=whole(1)[0],
        scratch_shapes=[pltpu.VMEM((NZ, 1, FB, grads.shape[1]), jnp.bfloat16), pltpu.SemaphoreType.DMA((NZ, 1))],
        out_shape=jax.ShapeDtypeStruct((2, 4, NB, TB, FB), jnp.bfloat16),
        compiler_params=pltpu.CompilerParams(vmem_limit_bytes=VMEM),
        name="spread_own",
    )(place, grads, weight)


def merge_kernel(one_ref, two_ref, *out_refs):
    for b in range(2):
        for i in range(4):
            both = one_ref[b, i].astype(jnp.float32) + two_ref[b, i].astype(jnp.float32)
            out_refs[4 * b + i][...] = both.astype(jnp.bfloat16)


def merge(one, two):
    shape = jax.ShapeDtypeStruct((NB, TB, FB), jnp.bfloat16)
    return pl.pallas_call(
        merge_kernel,
        in_specs=whole(2),
        out_specs=whole(8),
        out_shape=[shape] * 8,
        compiler_params=pltpu.CompilerParams(vmem_limit_bytes=VMEM),
        name="merge",
    )(one, two)


def total(parts):
    return functools.reduce(jnp.add, [p.astype(jnp.float32) for p in parts])


def per_device(enc_out, kv_weight, dec_query, ctx_grad, enc_seg, dec_seg):
    width = kv_weight.shape[3]
    place = jnp.stack([lax.axis_index(a) for a in AXES])

    near = small_stage(jnp.broadcast_to(enc_out, (NB, TB, FB)))
    far = across(near)
    own = [near] + [big_stage(near, i, -1) for i in (1, 2, 3)]
    far, own[1], kv_weight = lax.optimization_barrier((far, own[1], kv_weight))
    weight, mark = relayout(pltpu.with_memory_space_constraint(kv_weight, pltpu.HBM))
    weight = pltpu.with_memory_space_constraint(weight, pltpu.HBM)
    own += [far] + [big_stage(far, i, -1) for i in (1, 2, 3)]
    *own[:5], mark = lax.optimization_barrier((*own[:5], mark))
    other = [pltpu.with_memory_space_constraint(twin(v), pltpu.HBM) for v in own]

    enc_col = enc_seg.reshape(NB * TB, 1)
    context, grads, theirs = main(place, own, other, weight, mark, dec_query[0, 0], ctx_grad[0, 0], enc_col, dec_seg)
    theirs = twin(theirs)
    mine = spread_own(place, grads, weight)
    parts = merge(mine, theirs)
    away = [parts[4]] + [big_stage(parts[4 + i], i, 1) for i in (1, 2, 3)]
    home = [parts[0]] + [big_stage(parts[i], i, 1) for i in (1, 2, 3)]
    crossed = across(total(away).astype(jnp.bfloat16))
    planes = total(home + [crossed]).astype(jnp.bfloat16)
    owned = jnp.sum(small_stage(planes).astype(jnp.float32), axis=0)
    return context[None, None], owned[None]


def solution(mesh):
    fine = Mesh(mesh.devices.reshape(NZ, NC, NX, NY, ND), ("z", "c", "x", "y", "d"))
    section, mp = ("z", "c"), ("x", "y")
    placed = (
        P("d", mp, section),
        P(section, None, None, mp),
        P(section, "d", None, mp),
        P(section, "d", None, mp),
        P("d", None),
        P("d", None),
    )
    return jax.shard_map(
        per_device,
        mesh=fine,
        in_specs=placed,
        out_specs=(P(section, "d", None, mp), P("d", mp, section)),
        check_vma=False,
    )
```

time: 118 us -> 108 us (0.915)
  local copies, waits for them, and re-layouts: 10.3 us -> 1.73 us
  Pallas kernels: 22.2 us -> 27.3 us
  starting transfers between devices: 25.8 us -> 22 us
  waiting for transfers between devices: 32.7 us -> 30.7 us
    unnamed x9 -> x14, local copies, waits for them, and re-layouts: 9.42 us -> 0.81 us
    pallas_call x4 -> x3, Pallas kernels: 21.7 us -> 26.8 us  [the longest x1 14.3 us: main(): pl.pallas_call(main_kernel, in_specs=[SMEM] + whole(16) + [HBM] + whole(5...]
    ppermute x14, starting transfers between devices: 24 us -> 19.9 us  [joint(): return lax.ppermute(value, AXES, pairs)]
    ppermute x9, waiting for transfers between devices: 2.51 us -> 1.13 us  [twin(): return lax.ppermute(value, 'c', [(0, 1), (1, 0)])]
  transfers between devices with their start and end apart: 23 -> 23, of which waited for: 15 -> 11; matrix products, arithmetic and copies ran while one was open for 8% -> 0% of each run, Pallas kernels for 4% -> 12%
where the time goes in v1:
time: 108 us
  waiting for transfers between devices  30.7 us (28%)
  Pallas kernels  27.3 us (25%)
  blocking collectives  24.3 us (22%)
  starting transfers between devices  22 us (20%)
  local copies, waits for them, and re-layouts  1.73 us (2%)
    ppermute x14, waiting for transfers between devices, joint(): return lax.ppermute(value, AXES, pairs)  29.5 us
    all_to_all x2, blocking collectives, small_stage(): return lax.all_to_all(value, AXES, 0, 0, axis_index_groups=SMALL_GROUPS)  24.3 us
    ppermute x14, starting transfers between devices, joint(): return lax.ppermute(value, AXES, pairs)  19.9 us
    pallas_call x1, Pallas kernels, main(): pl.pallas_call(main_kernel, in_specs=[SMEM] + whole(16) + [HBM] + whole(5...  14.3 us
    pallas_call x1, Pallas kernels, relayout(): pl.pallas_call(relayout_kernel, in_specs=[HBM], out_specs=[HBM] + whole(1...  7.17 us
    pallas_call x1, Pallas kernels, spread_own(): pl.pallas_call(own_kernel, in_specs=[SMEM] + whole(1) + [HBM], out_specs=...  5.36 us
  transfers between devices with their start and end apart: 23, of which 11 were waited for; matrix products, arithmetic and copies ran while one was open for 0% of the time, Pallas kernels for 12%

profile of v1, /device:TPU:1, one launch (start us, length us, event | category | flops | bytes accessed | tf_op | source)
XLA Modules:
  0.0 107.8 jit_solution(16034736633012188228)
XLA Ops:
  0.6 0.8 broadcast_in_dim.14
  1.4 14.6 %all_to_all.10.refs_0_ = bf16[8,64,256]{2,1,0:T(8,128)(2,1)S(1)} all-to-all(bf16[8,64,256]{2,1,0:T(8,128)(2,1)S(1)} %broadcast_in_dim.14), channel_id=1, replica_groups={{0,32,64,96,128,160,192,224},{2,34,66,98,130,162,194,226},{4,36,68,100,..., dimensions={0} | all-to-all | bytes 524288 | tf_op jit(solution)/shard_map/all_to_all | solution.py:32
  16.0 5.7 %collective-permute-start.1 = (bf16[8,64,256]{2,1,0:T(8,128)(2,1)S(1)}, bf16[8,64,256]{2,1,0:T(8,128)(2,1)S(1)}, u32[]{:S(2)}, u32[]{:S(2)}) collective-permute-start(bf16[8,64,256]{2,1,0:T(8,128)(2,1)S(1)} %all_to_all.10.refs_0_), channel_id=1, source_target_pairs={{0,12},{2,14},{4,0},{6,2},{8,4},{10,6},{12,8},{14,10},{16,240},{18... | collective-permute-start | bytes 786440 | tf_op jit(solution)/shard_map/ppermute | solution.py:43
  21.6 1.4 %collective-permute-start = (bf16[8,64,256]{2,1,0:T(8,128)(2,1)S(1)}, bf16[8,64,256]{2,1,0:T(8,128)(2,1)S(1)}, u32[]{:S(2)}, u32[]{:S(2)}) collective-permute-start(bf16[8,64,256]{2,1,0:T(8,128)(2,1)S(1)} %all_to_all.10.refs_0_), channel_id=1, source_target_pairs={{0,2},{2,0},{4,6},{6,4},{8,10},{10,8},{12,14},{14,12},{16,144},{18... | collective-permute-start | bytes 786440 | tf_op jit(solution)/shard_map/ppermute | solution.py:43
  23.1 1.4 %collective-permute-start.3 = (bf16[8,64,256]{2,1,0:T(8,128)(2,1)S(1)}, bf16[8,64,256]{2,1,0:T(8,128)(2,1)S(1)}, u32[]{:S(2)}, u32[]{:S(2)}) collective-permute-start(bf16[8,64,256]{2,1,0:T(8,128)(2,1)S(1)} %all_to_all.10.refs_0_), channel_id=1, source_target_pairs={{0,4},{2,6},{4,8},{6,10},{8,12},{10,14},{12,0},{14,2},{16,48},{18,... | collective-permute-start | bytes 786440 | tf_op jit(solution)/shard_map/ppermute | solution.py:43
  24.4 0.5 collective-permute-done.1.refs_1_
  25.0 8.6 %collective-permute-done.refs_4_ = bf16[8,64,256]{2,1,0:T(8,128)(2,1)S(1)} collective-permute-done((bf16[8,64,256]{2,1,0:T(8,128)(2,1)S(1)}, bf16[8,64,256]{2,1,0:T(8,128)(2,1)S(1)}, u32[]{:S(2)}, u32[]{:S(2)}) %collective-permute-start) | collective-permute-done | bytes 262176 | tf_op jit(solution)/shard_map/ppermute | solution.py:43
  34.0 4.0 %collective-permute-start.5 = (bf16[8,64,256]{2,1,0:T(8,128)(2,1)S(1)}, bf16[8,64,256]{2,1,0:T(8,128)(2,1)S(1)}, u32[]{:S(2)}, u32[]{:S(2)}) collective-permute-start(bf16[8,64,256]{2,1,0:T(8,128)(2,1)S(1)} %collective-permute-done.refs_4_), channel_id=1, source_target_pairs={{0,8},{2,10},{4,12},{6,14},{8,0},{10,2},{12,4},{14,6},{16,208},{18... | collective-permute-start | bytes 786440 | tf_op jit(solution)/shard_map/ppermute | solution.py:43
  38.0 7.2 %relayout.1 = (bf16[8,2,256,1024]{3,2,1,0:T(8,128)(2,1)}, f32[8,128]{1,0:T(8,128)S(1)}) custom-call(bf16[1,4096,2,512]{3,2,1,0:T(2,128)(2,1)} %w_ref), custom_call_target="tpu_custom_call" | custom-call | tf_op jit(solution)/shard_map/relayout/pallas_call | solution.py:87
  46.3 0.6 collective-permute-done.4.refs_5_
  48.3 0.6 copy-done.5
  49.8 14.3 %main.1 = (bf16[512,512]{1,0:T(8,128)(2,1)}, bf16[512,1024]{1,0:T(8,128)(2,1)S(1)}, bf16[2,4,8,64,256]{4,3,2,1,0:T(8,128)(2,1)S(1)}) custom-call(s32[4]{0:T(128)S(1)} %pad_add_fusion.place_ref, bf16[8,64,256]{2,1,0:T(8,128)(2,1)S(1)} %all_to_all.10.refs_0_, bf16[8,64,256]{2,1,0:T(8,128)(2,1)S(1)} %collective-permute-done.1.refs_1_, ...), custom_call_target="tpu_custom_call" | custom-call | tf_op jit(solution)/shard_map/main/pallas_call | solution.py:200
  64.4 5.4 %spread_own.1.one_ref = bf16[2,4,8,64,256]{4,3,2,1,0:T(8,128)(2,1)S(1)} custom-call(s32[4]{0:T(128)S(1)} %pad_add_fusion.place_ref, bf16[512,1024]{1,0:T(8,128)(2,1)S(1)} %get-tuple-element.36.grad_ref, bf16[8,2,256,1024]{3,2,1,0:T(8,128)(2,1)} %get-tuple-element.33.refs_16_.w_ref), custom_call_target="tpu_custom_call" | custom-call | tf_op jit(solution)/shard_map/spread_own/pallas_call | solution.py:230
  70.2 1.3 %collective-permute-start.19 = (bf16[8,64,256]{2,1,0:T(8,128)(2,1)S(1)}, bf16[8,64,256]{2,1,0:T(8,128)(2,1)S(1)}, u32[]{:S(2)}, u32[]{:S(2)}) collective-permute-start(bf16[8,64,256]{2,1,0:T(8,128)(2,1)S(1)} %get-tuple-element.43), channel_id=1, source_target_pairs={{0,4},{2,6},{4,8},{6,10},{8,12},{10,14},{12,0},{14,2},{16,48},{18,... | collective-permute-start | bytes 786440 | tf_op jit(solution)/shard_map/ppermute | solution.py:43
  71.5 2.5 %collective-permute-start.21 = (bf16[8,64,256]{2,1,0:T(8,128)(2,1)S(1)}, bf16[8,64,256]{2,1,0:T(8,128)(2,1)S(1)}, u32[]{:S(2)}, u32[]{:S(2)}) collective-permute-start(bf16[8,64,256]{2,1,0:T(8,128)(2,1)S(1)} %get-tuple-element.45), channel_id=1, source_target_pairs={{0,12},{2,14},{4,0},{6,2},{8,4},{10,6},{12,8},{14,10},{16,240},{18... | collective-permute-start | bytes 786440 | tf_op jit(solution)/shard_map/ppermute | solution.py:43
  74.0 0.9 collective-permute-start.17
  74.9 2.6 %collective-permute-done.19 = bf16[8,64,256]{2,1,0:T(8,128)(2,1)S(1)} collective-permute-done((bf16[8,64,256]{2,1,0:T(8,128)(2,1)S(1)}, bf16[8,64,256]{2,1,0:T(8,128)(2,1)S(1)}, u32[]{:S(2)}, u32[]{:S(2)}) %collective-permute-start.19) | collective-permute-done | bytes 262176 | tf_op jit(solution)/shard_map/ppermute | solution.py:43
  77.5 2.2 %collective-permute-start.18 = (bf16[8,64,256]{2,1,0:T(8,128)(2,1)S(1)}, bf16[8,64,256]{2,1,0:T(8,128)(2,1)S(1)}, u32[]{:S(2)}, u32[]{:S(2)}) collective-permute-start(bf16[8,64,256]{2,1,0:T(8,128)(2,1)S(1)} %get-tuple-element.41), channel_id=1, source_target_pairs={{0,12},{2,14},{4,0},{6,2},{8,4},{10,6},{12,8},{14,10},{16,240},{18... | collective-permute-start | bytes 786440 | tf_op jit(solution)/shard_map/ppermute | solution.py:43
  79.6 4.6 %collective-permute-done.20 = bf16[8,64,256]{2,1,0:T(8,128)(2,1)S(1)} collective-permute-done((bf16[8,64,256]{2,1,0:T(8,128)(2,1)S(1)}, bf16[8,64,256]{2,1,0:T(8,128)(2,1)S(1)}, u32[]{:S(2)}, u32[]{:S(2)}) %collective-permute-start.20) | collective-permute-done | bytes 262176 | tf_op jit(solution)/shard_map/ppermute | solution.py:43
  84.6 1.3 %collective-permute-done.16 = bf16[8,64,256]{2,1,0:T(8,128)(2,1)S(1)} collective-permute-done((bf16[8,64,256]{2,1,0:T(8,128)(2,1)S(1)}, bf16[8,64,256]{2,1,0:T(8,128)(2,1)S(1)}, u32[]{:S(2)}, u32[]{:S(2)}) %collective-permute-start.16) | collective-permute-done | bytes 262176 | tf_op jit(solution)/shard_map/ppermute | solution.py:43
  85.9 6.7 %collective-permute-done.17 = bf16[8,64,256]{2,1,0:T(8,128)(2,1)S(1)} collective-permute-done((bf16[8,64,256]{2,1,0:T(8,128)(2,1)S(1)}, bf16[8,64,256]{2,1,0:T(8,128)(2,1)S(1)}, u32[]{:S(2)}, u32[]{:S(2)}) %collective-permute-start.17) | collective-permute-done | bytes 262176 | tf_op jit(solution)/shard_map/ppermute | solution.py:43
  92.6 4.6 %collective-permute-done.22 = bf16[8,64,256]{2,1,0:T(8,128)(2,1)S(1)} collective-permute-done((bf16[8,64,256]{2,1,0:T(8,128)(2,1)S(1)}, bf16[8,64,256]{2,1,0:T(8,128)(2,1)S(1)}, u32[]{:S(2)}, u32[]{:S(2)}) %collective-permute-start.22) | collective-permute-done | bytes 262176 | tf_op jit(solution)/shard_map/ppermute | solution.py:43
  97.4 9.7 %all_to_all.11 = bf16[8,64,256]{2,1,0:T(8,128)(2,1)S(1)} all-to-all(bf16[8,64,256]{2,1,0:T(8,128)(2,1)S(1)} %add_convert_fusion), channel_id=1, replica_groups={{0,32,64,96,128,160,192,224},{2,34,66,98,130,162,194,226},{4,36,68,100,..., dimensions={0} | all-to-all | bytes 524288 | tf_op jit(solution)/shard_map/all_to_all | solution.py:32
  107.1 0.7 convert_reduce_fusion
  (48 shorter events, 5.2 us)
Async XLA Ops:
  16.0 33.8 %copy-start.2 = (s32[1,512]{1,0:T(1,128)S(1)}, s32[1,512]{1,0:T(1,128)}, u32[]{:S(2)}) copy-start(s32[1,512]{1,0:T(1,128)} %refs_21_.1) | copy-start | bytes 6148
  16.0 9.0 %collective-permute-start.1 = (bf16[8,64,256]{2,1,0:T(8,128)(2,1)S(1)}, bf16[8,64,256]{2,1,0:T(8,128)(2,1)S(1)}, u32[]{:S(2)}, u32[]{:S(2)}) collective-permute-start(bf16[8,64,256]{2,1,0:T(8,128)(2,1)S(1)} %all_to_all.10.refs_0_), channel_id=1, source_target_pairs={{0,12},{2,14},{4,0},{6,2},{8,4},{10,6},{12,8},{14,10},{16,240},{18... | collective-permute-start | bytes 786440 | tf_op jit(solution)/shard_map/ppermute | solution.py:43
  21.6 11.9 %collective-permute-start = (bf16[8,64,256]{2,1,0:T(8,128)(2,1)S(1)}, bf16[8,64,256]{2,1,0:T(8,128)(2,1)S(1)}, u32[]{:S(2)}, u32[]{:S(2)}) collective-permute-start(bf16[8,64,256]{2,1,0:T(8,128)(2,1)S(1)} %all_to_all.10.refs_0_), channel_id=1, source_target_pairs={{0,2},{2,0},{4,6},{6,4},{8,10},{10,8},{12,14},{14,12},{16,144},{18... | collective-permute-start | bytes 786440 | tf_op jit(solution)/shard_map/ppermute | solution.py:43
  23.1 22.1 %collective-permute-start.3 = (bf16[8,64,256]{2,1,0:T(8,128)(2,1)S(1)}, bf16[8,64,256]{2,1,0:T(8,128)(2,1)S(1)}, u32[]{:S(2)}, u32[]{:S(2)}) collective-permute-start(bf16[8,64,256]{2,1,0:T(8,128)(2,1)S(1)} %all_to_all.10.refs_0_), channel_id=1, source_target_pairs={{0,4},{2,6},{4,8},{6,10},{8,12},{10,14},{12,0},{14,2},{16,48},{18,... | collective-permute-start | bytes 786440 | tf_op jit(solution)/shard_map/ppermute | solution.py:43
  24.4 20.7 %collective-permute-start.2 = (bf16[8,64,256]{2,1,0:T(8,128)(2,1)S(1)}, bf16[8,64,256]{2,1,0:T(8,128)(2,1)S(1)}, u32[]{:S(2)}, u32[]{:S(2)}) collective-permute-start(bf16[8,64,256]{2,1,0:T(8,128)(2,1)S(1)} %all_to_all.10.refs_0_), channel_id=1, source_target_pairs={{0,8},{2,10},{4,12},{6,14},{8,0},{10,2},{12,4},{14,6},{16,208},{18... | collective-permute-start | bytes 786440 | tf_op jit(solution)/shard_map/ppermute | solution.py:43
  33.5 12.3 %collective-permute-start.6 = (bf16[8,64,256]{2,1,0:T(8,128)(2,1)S(1)}, bf16[8,64,256]{2,1,0:T(8,128)(2,1)S(1)}, u32[]{:S(2)}, u32[]{:S(2)}) collective-permute-start(bf16[8,64,256]{2,1,0:T(8,128)(2,1)S(1)} %collective-permute-done.refs_4_), channel_id=1, source_target_pairs={{0,4},{2,6},{4,8},{6,10},{8,12},{10,14},{12,0},{14,2},{16,48},{18,... | collective-permute-start | bytes 786440 | tf_op jit(solution)/shard_map/ppermute | solution.py:43
  34.0 11.9 %collective-permute-start.5 = (bf16[8,64,256]{2,1,0:T(8,128)(2,1)S(1)}, bf16[8,64,256]{2,1,0:T(8,128)(2,1)S(1)}, u32[]{:S(2)}, u32[]{:S(2)}) collective-permute-start(bf16[8,64,256]{2,1,0:T(8,128)(2,1)S(1)} %collective-permute-done.refs_4_), channel_id=1, source_target_pairs={{0,8},{2,10},{4,12},{6,14},{8,0},{10,2},{12,4},{14,6},{16,208},{18... | collective-permute-start | bytes 786440 | tf_op jit(solution)/shard_map/ppermute | solution.py:43
  38.0 8.9 %collective-permute-start.4 = (bf16[8,64,256]{2,1,0:T(8,128)(2,1)S(1)}, bf16[8,64,256]{2,1,0:T(8,128)(2,1)S(1)}, u32[]{:S(2)}, u32[]{:S(2)}) collective-permute-start(bf16[8,64,256]{2,1,0:T(8,128)(2,1)S(1)} %collective-permute-done.refs_4_), channel_id=1, source_target_pairs={{0,12},{2,14},{4,0},{6,2},{8,4},{10,6},{12,8},{14,10},{16,240},{18... | collective-permute-start | bytes 786440 | tf_op jit(solution)/shard_map/ppermute | solution.py:43
  45.2 1.7 %collective-permute-start.7 = (bf16[8,64,256]{2,1,0:T(8,128)(2,1)S(1)}, bf16[8,64,256]{2,1,0:T(8,128)(2,1)S(1)}, u32[]{:S(2)}, u32[]{:S(2)}) collective-permute-start(bf16[8,64,256]{2,1,0:T(8,128)(2,1)S(1)} %all_to_all.10.refs_0_), channel_id=1, source_target_pairs={{0,16},{16,0},{1,17},{17,1},{2,18},{18,2},{3,19},{19,3},{4,20},{20... | collective-permute-start | bytes 786440 | tf_op jit(solution)/shard_map/ppermute | solution.py:55
  45.3 2.1 %collective-permute-start.8 = (bf16[8,64,256]{2,1,0:T(8,128)(2,1)S(1)}, bf16[8,64,256]{2,1,0:T(8,128)(2,1)S(1)}, u32[]{:S(2)}, u32[]{:S(2)}) collective-permute-start(bf16[8,64,256]{2,1,0:T(8,128)(2,1)S(1)} %collective-permute-done.1.refs_1_), channel_id=1, source_target_pairs={{0,16},{16,0},{1,17},{17,1},{2,18},{18,2},{3,19},{19,3},{4,20},{20... | collective-permute-start | bytes 786440 | tf_op jit(solution)/shard_map/ppermute | solution.py:55
  45.8 2.1 %collective-permute-start.9 = (bf16[8,64,256]{2,1,0:T(8,128)(2,1)S(1)}, bf16[8,64,256]{2,1,0:T(8,128)(2,1)S(1)}, u32[]{:S(2)}, u32[]{:S(2)}) collective-permute-start(bf16[8,64,256]{2,1,0:T(8,128)(2,1)S(1)} %collective-permute-done.2.refs_2_), channel_id=1, source_target_pairs={{0,16},{16,0},{1,17},{17,1},{2,18},{18,2},{3,19},{19,3},{4,20},{20... | collective-permute-start | bytes 786440 | tf_op jit(solution)/shard_map/ppermute | solution.py:55
  45.9 3.2 %collective-permute-start.10 = (bf16[8,64,256]{2,1,0:T(8,128)(2,1)S(1)}, bf16[8,64,256]{2,1,0:T(8,128)(2,1)}, u32[]{:S(2)}, u32[]{:S(2)}) collective-permute-start(bf16[8,64,256]{2,1,0:T(8,128)(2,1)S(1)} %collective-permute-done.3.refs_3_), channel_id=1, source_target_pairs={{0,16},{16,0},{1,17},{17,1},{2,18},{18,2},{3,19},{19,3},{4,20},{20... | collective-permute-start | bytes 786440 | tf_op jit(solution)/shard_map/ppermute | solution.py:55
  46.9 2.2 %collective-permute-start.11 = (bf16[8,64,256]{2,1,0:T(8,128)(2,1)S(1)}, bf16[8,64,256]{2,1,0:T(8,128)(2,1)}, u32[]{:S(2)}, u32[]{:S(2)}) collective-permute-start(bf16[8,64,256]{2,1,0:T(8,128)(2,1)S(1)} %collective-permute-done.refs_4_), channel_id=1, source_target_pairs={{0,16},{16,0},{1,17},{17,1},{2,18},{18,2},{3,19},{19,3},{4,20},{20... | collective-permute-start | bytes 786440 | tf_op jit(solution)/shard_map/ppermute | solution.py:55
  46.9 2.2 %collective-permute-start.14 = (bf16[8,64,256]{2,1,0:T(8,128)(2,1)S(1)}, bf16[8,64,256]{2,1,0:T(8,128)(2,1)}, u32[]{:S(2)}, u32[]{:S(2)}) collective-permute-start(bf16[8,64,256]{2,1,0:T(8,128)(2,1)S(1)} %collective-permute-done.6.refs_7_), channel_id=1, source_target_pairs={{0,16},{16,0},{1,17},{17,1},{2,18},{18,2},{3,19},{19,3},{4,20},{20... | collective-permute-start | bytes 786440 | tf_op jit(solution)/shard_map/ppermute | solution.py:55
  47.4 1.9 %collective-permute-start.13 = (bf16[8,64,256]{2,1,0:T(8,128)(2,1)S(1)}, bf16[8,64,256]{2,1,0:T(8,128)(2,1)}, u32[]{:S(2)}, u32[]{:S(2)}) collective-permute-start(bf16[8,64,256]{2,1,0:T(8,128)(2,1)S(1)} %collective-permute-done.5.refs_6_), channel_id=1, source_target_pairs={{0,16},{16,0},{1,17},{17,1},{2,18},{18,2},{3,19},{19,3},{4,20},{20... | collective-permute-start | bytes 786440 | tf_op jit(solution)/shard_map/ppermute | solution.py:55
  48.2 1.7 %collective-permute-start.12 = (bf16[8,64,256]{2,1,0:T(8,128)(2,1)S(1)}, bf16[8,64,256]{2,1,0:T(8,128)(2,1)}, u32[]{:S(2)}, u32[]{:S(2)}) collective-permute-start(bf16[8,64,256]{2,1,0:T(8,128)(2,1)S(1)} %collective-permute-done.4.refs_5_), channel_id=1, source_target_pairs={{0,16},{16,0},{1,17},{17,1},{2,18},{18,2},{3,19},{19,3},{4,20},{20... | collective-permute-start | bytes 786440 | tf_op jit(solution)/shard_map/ppermute | solution.py:55
  64.1 5.6 %collective-permute-start.15 = (bf16[2,4,8,64,256]{4,3,2,1,0:T(8,128)(2,1)S(1)}, bf16[2,4,8,64,256]{4,3,2,1,0:T(8,128)(2,1)S(1)}, u32[]{:S(2)}, u32[]{:S(2)}) collective-permute-start(bf16[2,4,8,64,256]{4,3,2,1,0:T(8,128)(2,1)S(1)} %get-tuple-element.37), channel_id=1, source_target_pairs={{0,16},{16,0},{1,17},{17,1},{2,18},{18,2},{3,19},{19,3},{4,20},{20... | collective-permute-start | bytes 6291464 | tf_op jit(solution)/shard_map/ppermute | solution.py:55
  70.2 7.2 %collective-permute-start.19 = (bf16[8,64,256]{2,1,0:T(8,128)(2,1)S(1)}, bf16[8,64,256]{2,1,0:T(8,128)(2,1)S(1)}, u32[]{:S(2)}, u32[]{:S(2)}) collective-permute-start(bf16[8,64,256]{2,1,0:T(8,128)(2,1)S(1)} %get-tuple-element.43), channel_id=1, source_target_pairs={{0,4},{2,6},{4,8},{6,10},{8,12},{10,14},{12,0},{14,2},{16,48},{18,... | collective-permute-start | bytes 786440 | tf_op jit(solution)/shard_map/ppermute | solution.py:43
  71.5 12.7 %collective-permute-start.20 = (bf16[8,64,256]{2,1,0:T(8,128)(2,1)S(1)}, bf16[8,64,256]{2,1,0:T(8,128)(2,1)S(1)}, u32[]{:S(2)}, u32[]{:S(2)}) collective-permute-start(bf16[8,64,256]{2,1,0:T(8,128)(2,1)S(1)} %get-tuple-element.44), channel_id=1, source_target_pairs={{0,8},{2,10},{4,12},{6,14},{8,0},{10,2},{12,4},{14,6},{16,80},{18,... | collective-permute-start | bytes 786440 | tf_op jit(solution)/shard_map/ppermute | solution.py:43
  71.5 12.7 %collective-permute-start.21 = (bf16[8,64,256]{2,1,0:T(8,128)(2,1)S(1)}, bf16[8,64,256]{2,1,0:T(8,128)(2,1)S(1)}, u32[]{:S(2)}, u32[]{:S(2)}) collective-permute-start(bf16[8,64,256]{2,1,0:T(8,128)(2,1)S(1)} %get-tuple-element.45), channel_id=1, source_target_pairs={{0,12},{2,14},{4,0},{6,2},{8,4},{10,6},{12,8},{14,10},{16,240},{18... | collective-permute-start | bytes 786440 | tf_op jit(solution)/shard_map/ppermute | solution.py:43
  74.0 11.9 %collective-permute-start.16 = (bf16[8,64,256]{2,1,0:T(8,128)(2,1)S(1)}, bf16[8,64,256]{2,1,0:T(8,128)(2,1)S(1)}, u32[]{:S(2)}, u32[]{:S(2)}) collective-permute-start(bf16[8,64,256]{2,1,0:T(8,128)(2,1)S(1)} %get-tuple-element.39), channel_id=1, source_target_pairs={{0,4},{2,6},{4,8},{6,10},{8,12},{10,14},{12,0},{14,2},{16,48},{18,... | collective-permute-start | bytes 786440 | tf_op jit(solution)/shard_map/ppermute | solution.py:43
  74.0 18.6 %collective-permute-start.17 = (bf16[8,64,256]{2,1,0:T(8,128)(2,1)S(1)}, bf16[8,64,256]{2,1,0:T(8,128)(2,1)S(1)}, u32[]{:S(2)}, u32[]{:S(2)}) collective-permute-start(bf16[8,64,256]{2,1,0:T(8,128)(2,1)S(1)} %get-tuple-element.40), channel_id=1, source_target_pairs={{0,8},{2,10},{4,12},{6,14},{8,0},{10,2},{12,4},{14,6},{16,80},{18,... | collective-permute-start | bytes 786440 | tf_op jit(solution)/shard_map/ppermute | solution.py:43
  77.5 15.1 %collective-permute-start.18 = (bf16[8,64,256]{2,1,0:T(8,128)(2,1)S(1)}, bf16[8,64,256]{2,1,0:T(8,128)(2,1)S(1)}, u32[]{:S(2)}, u32[]{:S(2)}) collective-permute-start(bf16[8,64,256]{2,1,0:T(8,128)(2,1)S(1)} %get-tuple-element.41), channel_id=1, source_target_pairs={{0,12},{2,14},{4,0},{6,2},{8,4},{10,6},{12,8},{14,10},{16,240},{18... | collective-permute-start | bytes 786440 | tf_op jit(solution)/shard_map/ppermute | solution.py:43
  84.4 12.8 %collective-permute-start.22 = (bf16[8,64,256]{2,1,0:T(8,128)(2,1)S(1)}, bf16[8,64,256]{2,1,0:T(8,128)(2,1)S(1)}, u32[]{:S(2)}, u32[]{:S(2)}) collective-permute-start(bf16[8,64,256]{2,1,0:T(8,128)(2,1)S(1)} %add_convert_fusion.1), channel_id=1, source_target_pairs={{0,2},{2,0},{4,6},{6,4},{8,10},{10,8},{12,14},{14,12},{16,144},{18... | collective-permute-start | bytes 786440 | tf_op jit(solution)/shard_map/ppermute | solution.py:43
  (6 other events, 104.0 us)

commit v2 on v1

--- a/solution.py
+++ b/solution.py
@@ -100,31 +100,32 @@
     )(weight)
 
 
-def lay_out(out_ref, parity, z, x, y, k, out):
-    @pl.when(parity == 0)
-    def _():
-        for m in range(NB):
-            out_ref[(m + y) % NY, (m // NY + NX - x) % NX, k] = out[m]
-
-    @pl.when(parity == 1)
-    def _():
-        away = (k + NZ - z) % NZ
-        i = away % 4
-        out_ref[(away // 4 + i // 3) % 2, i] = out
+def lay_out(out_refs, parity, z, x, y, k, out):
+    slot = (k + NZ - z) % NZ
+    i = slot % 4
+    b = (slot // 4 + i // 3) % 2
+    for half in range(2):
+
+        @pl.when((parity == 0) & (y == half))
+        def _():
+            for m in range(NB):
+                out_refs[(m + half) % NY][(m // NY + NX - x) % NX, k] = out[m]
+
+        @pl.when((parity == 1) & (b == half))
+        def _():
+            out_refs[half][i] = out
 
 
 def load_weights(w_ref, w_buf, sems, k, core, slot):
     return pltpu.make_async_copy(w_ref.at[k, core], w_buf.at[k, slot], sems.at[k, slot])
 
 
-def spread(grads, w_buf, slot, out_ref, parity, z, x, y, ready):
+def spread(grads, w_buf, slot, out_refs, parity, z, x, y):
     for k in range(0, NZ, 2):
-        ready(k)
-        ready(k + 1)
         rows = w_buf[pl.ds(k, 2), slot].reshape(2 * FB, grads.shape[1])
         out = lax.dot_general(grads, rows, NT, preferred_element_type=jnp.float32).astype(jnp.bfloat16)
         for n in range(2):
-            lay_out(out_ref, parity, z, x, y, k + n, out[:, n * FB:(n + 1) * FB].reshape(NB, TB, FB))
+            lay_out(out_refs, parity, z, x, y, k + n, out[:, n * FB:(n + 1) * FB].reshape(NB, TB, FB))
 
 
 def attend(q, g, k, v, same):
@@ -146,7 +147,7 @@
 
 def main_kernel(place_ref, *refs):
     own, other = refs[:8], refs[8:16]
-    w_ref, _, q_ref, g_ref, es_ref, ds_ref, ctx_ref, grad_ref, out_ref, w_buf, lhs_ref, acc_ref, kv_ref, sems = refs[16:]
+    w_ref, _, q_ref, g_ref, es_ref, ds_ref, ctx_ref, grad_ref, home_ref, away_ref, w_buf, lhs_ref, acc_ref, kv_ref, sems = refs[16:]
     z, core, x, y = place_ref[0], place_ref[1], place_ref[2], place_ref[3]
     dec, width = q_ref.shape
     enc = NB * TB
@@ -191,7 +192,7 @@
         found = attend(q_ref[:, head], g_ref[:, head], kv_ref[:, head], kv_ref[:, value], same)
         ctx_ref[:, head], grad_ref[:, head], grad_ref[:, value] = found
 
-    spread(grad_ref[...], w_buf, 1 - core, out_ref, 1 - core, z, x, y, lambda k: None)
+    spread(grad_ref[...], w_buf, 1 - core, (home_ref, away_ref), 1 - core, z, x, y)
 
 
 def main(place, own, other, weight, mark, query, grad, enc_col, dec_row):
@@ -200,7 +201,7 @@
     return pl.pallas_call(
         main_kernel,
         in_specs=[SMEM] + whole(16) + [HBM] + whole(5),
-        out_specs=whole(3),
+        out_specs=whole(4),
         scratch_shapes=[
             pltpu.VMEM((NZ, NC, FB, 2 * width), jnp.bfloat16),
             pltpu.VMEM((2 * NZ, enc, FB), jnp.bfloat16),
@@ -211,38 +212,58 @@
         out_shape=[
             jax.ShapeDtypeStruct((dec, width), jnp.bfloat16),
             jax.ShapeDtypeStruct((enc, 2 * width), jnp.bfloat16),
-            jax.ShapeDtypeStruct((2, 4, NB, TB, FB), jnp.bfloat16),
+            jax.ShapeDtypeStruct((4, NB, TB, FB), jnp.bfloat16),
+            jax.ShapeDtypeStruct((4, NB, TB, FB), jnp.bfloat16),
         ],
         compiler_params=pltpu.CompilerParams(vmem_limit_bytes=28 << 20),
         name="main",
     )(place, *own, *other, weight, mark, query, grad, enc_col, dec_row)
 
 
-def own_kernel(place_ref, grad_ref, w_ref, out_ref, w_buf, sems):
+def own_kernel(b, place_ref, grad_ref, w_ref, put):
     z, core, x, y = place_ref[0], place_ref[1], place_ref[2], place_ref[3]
-    for k in range(NZ):
-        load_weights(w_ref, w_buf, sems, k, core, 0).start()
-    ready = lambda k: load_weights(w_ref, w_buf, sems, k, core, 0).wait()
-    spread(grad_ref[...], w_buf, 0, out_ref, core, z, x, y, ready)
-
-
-def spread_own(place, grads, weight):
+
+    @pl.when(core == 0)
+    def _():
+        starts = [pl.multiple_of((NY * j + (y + b) % NY) * TB, TB) for j in range(NX)]
+        grads = jnp.concatenate([grad_ref[pl.ds(start, TB), :] for start in starts], axis=0)
+        for k in range(0, NZ, 2):
+            rows = w_ref[pl.ds(k, 2), 0].reshape(2 * FB, grads.shape[1])
+            out = lax.dot_general(grads, rows, NT, preferred_element_type=jnp.float32)
+            for j in range(NX):
+                for n in range(2):
+                    put((j + NX - x) % NX, k + n, out[j * TB:(j + 1) * TB, n * FB:(n + 1) * FB])
+
+    @pl.when(core == 1)
+    def _():
+        for i in range(0, 4, 2):
+            rows = [w_ref[(z + Z_STEP[i + n] + 4 * b) % NZ, 1] for n in range(2)]
+            out = lax.dot_general(grad_ref[...], jnp.concatenate(rows, axis=0), NT, preferred_element_type=jnp.float32)
+            for n in range(2):
+                put(i + n, slice(None), out[:, n * FB:(n + 1) * FB].reshape(NB, TB, FB))
+
+
+def plain_kernel(b, place_ref, grad_ref, w_ref, out_ref):
+    def put(i, k, value):
+        out_ref[i, k] = value.astype(jnp.bfloat16)
+
+    own_kernel(b, place_ref, grad_ref, w_ref, put)
+
+
+def spread_own(b, place, grads, weight):
     return pl.pallas_call(
-        own_kernel,
-        in_specs=[SMEM] + whole(1) + [HBM],
+        functools.partial(plain_kernel, b),
+        in_specs=[SMEM] + whole(2),
         out_specs=whole(1)[0],
-        scratch_shapes=[pltpu.VMEM((NZ, 1, FB, grads.shape[1]), jnp.bfloat16), pltpu.SemaphoreType.DMA((NZ, 1))],
-        out_shape=jax.ShapeDtypeStruct((2, 4, NB, TB, FB), jnp.bfloat16),
+        out_shape=jax.ShapeDtypeStruct((4, NB, TB, FB), jnp.bfloat16),
         compiler_params=pltpu.CompilerParams(vmem_limit_bytes=VMEM),
         name="spread_own",
     )(place, grads, weight)
 
 
 def merge_kernel(one_ref, two_ref, *out_refs):
-    for b in range(2):
-        for i in range(4):
-            both = one_ref[b, i].astype(jnp.float32) + two_ref[b, i].astype(jnp.float32)
-            out_refs[4 * b + i][...] = both.astype(jnp.bfloat16)
+    for i in range(4):
+        out_refs[i][...] = (one_ref[i].astype(jnp.float32) + two_ref[i].astype(jnp.float32)).astype(jnp.bfloat16)
 
 
 def merge(one, two):
@@ -250,8 +271,8 @@
     return pl.pallas_call(
         merge_kernel,
         in_specs=whole(2),
-        out_specs=whole(8),
-        out_shape=[shape] * 8,
+        out_specs=whole(4),
+        out_shape=[shape] * 4,
         compiler_params=pltpu.CompilerParams(vmem_limit_bytes=VMEM),
         name="merge",
     )(one, two)
@@ -268,20 +289,21 @@
     near = small_stage(jnp.broadcast_to(enc_out, (NB, TB, FB)))
     far = across(near)
     own = [near] + [big_stage(near, i, -1) for i in (1, 2, 3)]
-    far, own[1], kv_weight = lax.optimization_barrier((far, own[1], kv_weight))
+    own[1], far, kv_weight = lax.optimization_barrier((own[1], far, kv_weight))
     weight, mark = relayout(pltpu.with_memory_space_constraint(kv_weight, pltpu.HBM))
-    weight = pltpu.with_memory_space_constraint(weight, pltpu.HBM)
+    held = pltpu.with_memory_space_constraint(weight, pltpu.HBM)
     own += [far] + [big_stage(far, i, -1) for i in (1, 2, 3)]
     *own[:5], mark = lax.optimization_barrier((*own[:5], mark))
     other = [pltpu.with_memory_space_constraint(twin(v), pltpu.HBM) for v in own]
 
     enc_col = enc_seg.reshape(NB * TB, 1)
-    context, grads, theirs = main(place, own, other, weight, mark, dec_query[0, 0], ctx_grad[0, 0], enc_col, dec_seg)
-    theirs = twin(theirs)
-    mine = spread_own(place, grads, weight)
-    parts = merge(mine, theirs)
-    away = [parts[4]] + [big_stage(parts[4 + i], i, 1) for i in (1, 2, 3)]
-    home = [parts[0]] + [big_stage(parts[i], i, 1) for i in (1, 2, 3)]
+    context, grads, home, away = main(place, own, other, held, mark, dec_query[0, 0], ctx_grad[0, 0], enc_col, dec_seg)
+    away, home = twin(away), twin(home)
+    away = merge(spread_own(1, place, grads, weight), away)
+    *away, late = lax.optimization_barrier((*away, grads))
+    away = [away[0]] + [big_stage(away[i], i, 1) for i in (1, 2, 3)]
+    home = merge(spread_own(0, place, late, weight), home)
+    home = [home[0]] + [big_stage(home[i], i, 1) for i in (1, 2, 3)]
     crossed = across(total(away).astype(jnp.bfloat16))
     planes = total(home + [crossed]).astype(jnp.bfloat16)
     owned = jnp.sum(small_stage(planes).astype(jnp.float32), axis=0)

time: 108 us -> 106 us (0.981)
  starting transfers between devices: 22 us -> 18.9 us
    ppermute x14, starting transfers between devices: 19.9 us -> 15.8 us  [joint(): return lax.ppermute(value, AXES, pairs)]
    pallas_call x2 -> x4, Pallas kernels: 5.84 us -> 4.39 us  [the longest x2 3.91 us: spread_own(): pl.pallas_call(functools.partial(plain_kernel, b), in_specs=[SMEM] + whol...]
    ppermute x9 -> x10, starting transfers between devices: 2.1 us -> 3.12 us  [twin(): return lax.ppermute(value, 'c', [(0, 1), (1, 0)])]
  transfers between devices with their start and end apart: 23 -> 24, of which waited for: 11 -> 11; matrix products, arithmetic and copies ran while one was open for 0% -> 0% of each run, Pallas kernels for 12% -> 11%
where the time goes in v2:
time: 106 us; the launch traced here: 105 us
  waiting for transfers between devices  30.9 us (29%)
  Pallas kernels  26.5 us (25%)
  blocking collectives  24.9 us (23%)
  starting transfers between devices  18.9 us (18%)
  local copies, waits for them, and re-layouts  2.21 us (2%)
  other arithmetic  1.08 us (1%)
    ppermute x14, waiting for transfers between devices, joint(): return lax.ppermute(value, AXES, pairs)  30.1 us
    all_to_all x2, blocking collectives, small_stage(): return lax.all_to_all(value, AXES, 0, 0, axis_index_groups=SMALL_GROUPS)  24.9 us
    ppermute x14, starting transfers between devices, joint(): return lax.ppermute(value, AXES, pairs)  15.8 us
    pallas_call x1, Pallas kernels, main(): pl.pallas_call(main_kernel, in_specs=[SMEM] + whole(16) + [HBM] + whole(5...  15 us
    pallas_call x1, Pallas kernels, relayout(): pl.pallas_call(relayout_kernel, in_specs=[HBM], out_specs=[HBM] + whole(1...  7.17 us
    pallas_call x2, Pallas kernels, spread_own(): pl.pallas_call(functools.partial(plain_kernel, b), in_specs=[SMEM] + whol...  3.91 us
    ppermute x10, starting transfers between devices, twin(): return lax.ppermute(value, 'c', [(0, 1), (1, 0)])  3.12 us
  transfers between devices with their start and end apart: 24, of which 11 were waited for; matrix products, arithmetic and copies ran while one was open for 0% of the time, Pallas kernels for 11%

profile of v2, /device:TPU:1, one launch (start us, length us, event | category | flops | bytes accessed | tf_op | source)
XLA Modules:
  0.0 105.4 jit_solution(12932036026790471357)
XLA Ops:
  0.7 0.9 broadcast_in_dim.14
  1.5 14.6 %all_to_all.10.refs_0_ = bf16[8,64,256]{2,1,0:T(8,128)(2,1)S(1)} all-to-all(bf16[8,64,256]{2,1,0:T(8,128)(2,1)S(1)} %broadcast_in_dim.14), channel_id=1, replica_groups={{0,32,64,96,128,160,192,224},{2,34,66,98,130,162,194,226},{4,36,68,100,..., dimensions={0} | all-to-all | bytes 524288 | tf_op jit(solution)/shard_map/all_to_all | solution.py:32
  16.1 6.9 %collective-permute-start.1 = (bf16[8,64,256]{2,1,0:T(8,128)(2,1)S(1)}, bf16[8,64,256]{2,1,0:T(8,128)(2,1)S(1)}, u32[]{:S(2)}, u32[]{:S(2)}) collective-permute-start(bf16[8,64,256]{2,1,0:T(8,128)(2,1)S(1)} %all_to_all.10.refs_0_), channel_id=1, source_target_pairs={{0,2},{2,0},{4,6},{6,4},{8,10},{10,8},{12,14},{14,12},{16,144},{18... | collective-permute-start | bytes 786440 | tf_op jit(solution)/shard_map/ppermute | solution.py:43
  23.0 1.5 %collective-permute-start.3 = (bf16[8,64,256]{2,1,0:T(8,128)(2,1)S(1)}, bf16[8,64,256]{2,1,0:T(8,128)(2,1)S(1)}, u32[]{:S(2)}, u32[]{:S(2)}) collective-permute-start(bf16[8,64,256]{2,1,0:T(8,128)(2,1)S(1)} %all_to_all.10.refs_0_), channel_id=1, source_target_pairs={{0,4},{2,6},{4,8},{6,10},{8,12},{10,14},{12,0},{14,2},{16,48},{18,... | collective-permute-start | bytes 786440 | tf_op jit(solution)/shard_map/ppermute | solution.py:43
  24.5 2.5 %collective-permute-done.1.refs_4_ = bf16[8,64,256]{2,1,0:T(8,128)(2,1)S(1)} collective-permute-done((bf16[8,64,256]{2,1,0:T(8,128)(2,1)S(1)}, bf16[8,64,256]{2,1,0:T(8,128)(2,1)S(1)}, u32[]{:S(2)}, u32[]{:S(2)}) %collective-permute-start.1) | collective-permute-done | bytes 262176 | tf_op jit(solution)/shard_map/ppermute | solution.py:43
  26.9 6.7 %collective-permute-done.refs_1_ = bf16[8,64,256]{2,1,0:T(8,128)(2,1)S(1)} collective-permute-done((bf16[8,64,256]{2,1,0:T(8,128)(2,1)S(1)}, bf16[8,64,256]{2,1,0:T(8,128)(2,1)S(1)}, u32[]{:S(2)}, u32[]{:S(2)}) %collective-permute-start) | collective-permute-done | bytes 262176 | tf_op jit(solution)/shard_map/ppermute | solution.py:43
  33.6 2.9 %collective-permute-start.5 = (bf16[8,64,256]{2,1,0:T(8,128)(2,1)S(1)}, bf16[8,64,256]{2,1,0:T(8,128)(2,1)S(1)}, u32[]{:S(2)}, u32[]{:S(2)}) collective-permute-start(bf16[8,64,256]{2,1,0:T(8,128)(2,1)S(1)} %collective-permute-done.1.refs_4_), channel_id=1, source_target_pairs={{0,8},{2,10},{4,12},{6,14},{8,0},{10,2},{12,4},{14,6},{16,208},{18... | collective-permute-start | bytes 786440 | tf_op jit(solution)/shard_map/ppermute | solution.py:43
  36.5 7.2 %relayout.1 = (bf16[8,2,256,1024]{3,2,1,0:T(8,128)(2,1)}, f32[8,128]{1,0:T(8,128)S(1)}) custom-call(bf16[1,4096,2,512]{3,2,1,0:T(2,128)(2,1)} %w_ref), custom_call_target="tpu_custom_call" | custom-call | tf_op jit(solution)/shard_map/relayout/pallas_call | solution.py:87
  43.8 1.2 %collective-permute-start.7 = (bf16[8,64,256]{2,1,0:T(8,128)(2,1)S(1)}, bf16[8,64,256]{2,1,0:T(8,128)(2,1)S(1)}, u32[]{:S(2)}, u32[]{:S(2)}) collective-permute-start(bf16[8,64,256]{2,1,0:T(8,128)(2,1)S(1)} %all_to_all.10.refs_0_), channel_id=1, source_target_pairs={{0,16},{16,0},{1,17},{17,1},{2,18},{18,2},{3,19},{19,3},{4,20},{20... | collective-permute-start | bytes 786440 | tf_op jit(solution)/shard_map/ppermute | solution.py:55
  45.5 1.8 %collective-permute-done.4.refs_5_ = bf16[8,64,256]{2,1,0:T(8,128)(2,1)S(1)} collective-permute-done((bf16[8,64,256]{2,1,0:T(8,128)(2,1)S(1)}, bf16[8,64,256]{2,1,0:T(8,128)(2,1)S(1)}, u32[]{:S(2)}, u32[]{:S(2)}) %collective-permute-start.4) | collective-permute-done | bytes 262176 | tf_op jit(solution)/shard_map/ppermute | solution.py:43
  47.9 0.6 copy-done.5
  48.7 0.6 copy-done.6
  50.2 15.0 %main.1 = (bf16[512,512]{1,0:T(8,128)(2,1)}, bf16[512,1024]{1,0:T(8,128)(2,1)S(1)}, bf16[4,8,64,256]{3,2,1,0:T(8,128)(2,1)S(1)}, bf16[4,8,64,256]{3,2,1,0:T(8,128)(2,1)S(1)}) custom-call(s32[4]{0:T(128)S(1)} %pad_add_fusion.place_ref, bf16[8,64,256]{2,1,0:T(8,128)(2,1)S(1)} %all_to_all.10.refs_0_, bf16[8,64,256]{2,1,0:T(8,128)(2,1)S(1)} %collective-permute-done.refs_1_, ...), custom_call_target="tpu_custom_call" | custom-call | tf_op jit(solution)/shard_map/main/pallas_call | solution.py:201
  65.8 2.1 %spread_own.2.one_ref = bf16[4,8,64,256]{3,2,1,0:T(8,128)(2,1)S(1)} custom-call(s32[4]{0:T(128)S(1)} %pad_add_fusion.place_ref, bf16[512,1024]{1,0:T(8,128)(2,1)S(1)} %get-tuple-element.48.grad_ref, bf16[8,2,256,1024]{3,2,1,0:T(8,128)(2,1)S(1)} %copy-done), custom_call_target="tpu_custom_call" | custom-call | tf_op jit(solution)/shard_map/spread_own/pallas_call | solution.py:254
  68.5 2.6 %collective-permute-start.22 = (bf16[8,64,256]{2,1,0:T(8,128)(2,1)S(1)}, bf16[8,64,256]{2,1,0:T(8,128)(2,1)S(1)}, u32[]{:S(2)}, u32[]{:S(2)}) collective-permute-start(bf16[8,64,256]{2,1,0:T(8,128)(2,1)S(1)} %get-tuple-element.57), channel_id=1, source_target_pairs={{0,12},{2,14},{4,0},{6,2},{8,4},{10,6},{12,8},{14,10},{16,240},{18... | collective-permute-start | bytes 786440 | tf_op jit(solution)/shard_map/ppermute | solution.py:43
  71.0 1.8 %spread_own.3.one_ref = bf16[4,8,64,256]{3,2,1,0:T(8,128)(2,1)S(1)} custom-call(s32[4]{0:T(128)S(1)} %pad_add_fusion.place_ref, bf16[512,1024]{1,0:T(8,128)(2,1)S(1)} %get-tuple-element.48.grad_ref, bf16[8,2,256,1024]{3,2,1,0:T(8,128)(2,1)S(1)} %copy-done), custom_call_target="tpu_custom_call" | custom-call | tf_op jit(solution)/shard_map/spread_own/pallas_call | solution.py:254
  73.8 1.3 %collective-permute-done.20 = bf16[8,64,256]{2,1,0:T(8,128)(2,1)S(1)} collective-permute-done((bf16[8,64,256]{2,1,0:T(8,128)(2,1)S(1)}, bf16[8,64,256]{2,1,0:T(8,128)(2,1)S(1)}, u32[]{:S(2)}, u32[]{:S(2)}) %collective-permute-start.20) | collective-permute-done | bytes 262176 | tf_op jit(solution)/shard_map/ppermute | solution.py:43
  75.0 1.0 collective-permute-start.19
  76.0 5.0 %collective-permute-done.21 = bf16[8,64,256]{2,1,0:T(8,128)(2,1)S(1)} collective-permute-done((bf16[8,64,256]{2,1,0:T(8,128)(2,1)S(1)}, bf16[8,64,256]{2,1,0:T(8,128)(2,1)S(1)}, u32[]{:S(2)}, u32[]{:S(2)}) %collective-permute-start.21) | collective-permute-done | bytes 262176 | tf_op jit(solution)/shard_map/ppermute | solution.py:43
  81.3 2.2 %collective-permute-done.17 = bf16[8,64,256]{2,1,0:T(8,128)(2,1)S(1)} collective-permute-done((bf16[8,64,256]{2,1,0:T(8,128)(2,1)S(1)}, bf16[8,64,256]{2,1,0:T(8,128)(2,1)S(1)}, u32[]{:S(2)}, u32[]{:S(2)}) %collective-permute-start.17) | collective-permute-done | bytes 262176 | tf_op jit(solution)/shard_map/ppermute | solution.py:43
  83.4 5.9 %collective-permute-done.18 = bf16[8,64,256]{2,1,0:T(8,128)(2,1)S(1)} collective-permute-done((bf16[8,64,256]{2,1,0:T(8,128)(2,1)S(1)}, bf16[8,64,256]{2,1,0:T(8,128)(2,1)S(1)}, u32[]{:S(2)}, u32[]{:S(2)}) %collective-permute-start.18) | collective-permute-done | bytes 262176 | tf_op jit(solution)/shard_map/ppermute | solution.py:43
  89.3 4.9 %collective-permute-done.23 = bf16[8,64,256]{2,1,0:T(8,128)(2,1)S(1)} collective-permute-done((bf16[8,64,256]{2,1,0:T(8,128)(2,1)S(1)}, bf16[8,64,256]{2,1,0:T(8,128)(2,1)S(1)}, u32[]{:S(2)}, u32[]{:S(2)}) %collective-permute-start.23) | collective-permute-done | bytes 262176 | tf_op jit(solution)/shard_map/ppermute | solution.py:43
  94.4 10.3 %all_to_all.11 = bf16[8,64,256]{2,1,0:T(8,128)(2,1)S(1)} all-to-all(bf16[8,64,256]{2,1,0:T(8,128)(2,1)S(1)} %add_convert_fusion), channel_id=1, replica_groups={{0,32,64,96,128,160,192,224},{2,34,66,98,130,162,194,226},{4,36,68,100,..., dimensions={0} | all-to-all | bytes 524288 | tf_op jit(solution)/shard_map/all_to_all | solution.py:32
  104.8 0.7 convert_reduce_fusion
  (54 shorter events, 4.8 us)
Async XLA Ops:
  16.1 10.8 %collective-permute-start.1 = (bf16[8,64,256]{2,1,0:T(8,128)(2,1)S(1)}, bf16[8,64,256]{2,1,0:T(8,128)(2,1)S(1)}, u32[]{:S(2)}, u32[]{:S(2)}) collective-permute-start(bf16[8,64,256]{2,1,0:T(8,128)(2,1)S(1)} %all_to_all.10.refs_0_), channel_id=1, source_target_pairs={{0,2},{2,0},{4,6},{6,4},{8,10},{10,8},{12,14},{14,12},{16,144},{18... | collective-permute-start | bytes 786440 | tf_op jit(solution)/shard_map/ppermute | solution.py:43
  23.0 10.6 %collective-permute-start = (bf16[8,64,256]{2,1,0:T(8,128)(2,1)S(1)}, bf16[8,64,256]{2,1,0:T(8,128)(2,1)S(1)}, u32[]{:S(2)}, u32[]{:S(2)}) collective-permute-start(bf16[8,64,256]{2,1,0:T(8,128)(2,1)S(1)} %all_to_all.10.refs_0_), channel_id=1, source_target_pairs={{0,12},{2,14},{4,0},{6,2},{8,4},{10,6},{12,8},{14,10},{16,240},{18... | collective-permute-start | bytes 786440 | tf_op jit(solution)/shard_map/ppermute | solution.py:43
  23.0 20.7 %collective-permute-start.3 = (bf16[8,64,256]{2,1,0:T(8,128)(2,1)S(1)}, bf16[8,64,256]{2,1,0:T(8,128)(2,1)S(1)}, u32[]{:S(2)}, u32[]{:S(2)}) collective-permute-start(bf16[8,64,256]{2,1,0:T(8,128)(2,1)S(1)} %all_to_all.10.refs_0_), channel_id=1, source_target_pairs={{0,4},{2,6},{4,8},{6,10},{8,12},{10,14},{12,0},{14,2},{16,48},{18,... | collective-permute-start | bytes 786440 | tf_op jit(solution)/shard_map/ppermute | solution.py:43
  24.5 19.3 %collective-permute-start.2 = (bf16[8,64,256]{2,1,0:T(8,128)(2,1)S(1)}, bf16[8,64,256]{2,1,0:T(8,128)(2,1)S(1)}, u32[]{:S(2)}, u32[]{:S(2)}) collective-permute-start(bf16[8,64,256]{2,1,0:T(8,128)(2,1)S(1)} %all_to_all.10.refs_0_), channel_id=1, source_target_pairs={{0,8},{2,10},{4,12},{6,14},{8,0},{10,2},{12,4},{14,6},{16,208},{18... | collective-permute-start | bytes 786440 | tf_op jit(solution)/shard_map/ppermute | solution.py:43
  33.6 11.4 %collective-permute-start.6 = (bf16[8,64,256]{2,1,0:T(8,128)(2,1)S(1)}, bf16[8,64,256]{2,1,0:T(8,128)(2,1)S(1)}, u32[]{:S(2)}, u32[]{:S(2)}) collective-permute-start(bf16[8,64,256]{2,1,0:T(8,128)(2,1)S(1)} %collective-permute-done.1.refs_4_), channel_id=1, source_target_pairs={{0,4},{2,6},{4,8},{6,10},{8,12},{10,14},{12,0},{14,2},{16,48},{18,... | collective-permute-start | bytes 786440 | tf_op jit(solution)/shard_map/ppermute | solution.py:43
  33.6 11.8 %collective-permute-start.5 = (bf16[8,64,256]{2,1,0:T(8,128)(2,1)S(1)}, bf16[8,64,256]{2,1,0:T(8,128)(2,1)S(1)}, u32[]{:S(2)}, u32[]{:S(2)}) collective-permute-start(bf16[8,64,256]{2,1,0:T(8,128)(2,1)S(1)} %collective-permute-done.1.refs_4_), channel_id=1, source_target_pairs={{0,8},{2,10},{4,12},{6,14},{8,0},{10,2},{12,4},{14,6},{16,208},{18... | collective-permute-start | bytes 786440 | tf_op jit(solution)/shard_map/ppermute | solution.py:43
  36.5 10.8 %collective-permute-start.4 = (bf16[8,64,256]{2,1,0:T(8,128)(2,1)S(1)}, bf16[8,64,256]{2,1,0:T(8,128)(2,1)S(1)}, u32[]{:S(2)}, u32[]{:S(2)}) collective-permute-start(bf16[8,64,256]{2,1,0:T(8,128)(2,1)S(1)} %collective-permute-done.1.refs_4_), channel_id=1, source_target_pairs={{0,12},{2,14},{4,0},{6,2},{8,4},{10,6},{12,8},{14,10},{16,240},{18... | collective-permute-start | bytes 786440 | tf_op jit(solution)/shard_map/ppermute | solution.py:43
  43.8 3.6 %collective-permute-start.7 = (bf16[8,64,256]{2,1,0:T(8,128)(2,1)S(1)}, bf16[8,64,256]{2,1,0:T(8,128)(2,1)S(1)}, u32[]{:S(2)}, u32[]{:S(2)}) collective-permute-start(bf16[8,64,256]{2,1,0:T(8,128)(2,1)S(1)} %all_to_all.10.refs_0_), channel_id=1, source_target_pairs={{0,16},{16,0},{1,17},{17,1},{2,18},{18,2},{3,19},{19,3},{4,20},{20... | collective-permute-start | bytes 786440 | tf_op jit(solution)/shard_map/ppermute | solution.py:55
  44.9 2.9 %collective-permute-start.8 = (bf16[8,64,256]{2,1,0:T(8,128)(2,1)S(1)}, bf16[8,64,256]{2,1,0:T(8,128)(2,1)S(1)}, u32[]{:S(2)}, u32[]{:S(2)}) collective-permute-start(bf16[8,64,256]{2,1,0:T(8,128)(2,1)S(1)} %collective-permute-done.refs_1_), channel_id=1, source_target_pairs={{0,16},{16,0},{1,17},{17,1},{2,18},{18,2},{3,19},{19,3},{4,20},{20... | collective-permute-start | bytes 786440 | tf_op jit(solution)/shard_map/ppermute | solution.py:55
  45.0 2.9 %collective-permute-start.9 = (bf16[8,64,256]{2,1,0:T(8,128)(2,1)S(1)}, bf16[8,64,256]{2,1,0:T(8,128)(2,1)S(1)}, u32[]{:S(2)}, u32[]{:S(2)}) collective-permute-start(bf16[8,64,256]{2,1,0:T(8,128)(2,1)S(1)} %collective-permute-done.2.refs_2_), channel_id=1, source_target_pairs={{0,16},{16,0},{1,17},{17,1},{2,18},{18,2},{3,19},{19,3},{4,20},{20... | collective-permute-start | bytes 786440 | tf_op jit(solution)/shard_map/ppermute | solution.py:55
  45.4 4.1 %collective-permute-start.10 = (bf16[8,64,256]{2,1,0:T(8,128)(2,1)S(1)}, bf16[8,64,256]{2,1,0:T(8,128)(2,1)}, u32[]{:S(2)}, u32[]{:S(2)}) collective-permute-start(bf16[8,64,256]{2,1,0:T(8,128)(2,1)S(1)} %collective-permute-done.3.refs_3_), channel_id=1, source_target_pairs={{0,16},{16,0},{1,17},{17,1},{2,18},{18,2},{3,19},{19,3},{4,20},{20... | collective-permute-start | bytes 786440 | tf_op jit(solution)/shard_map/ppermute | solution.py:55
  47.3 2.2 %collective-permute-start.11 = (bf16[8,64,256]{2,1,0:T(8,128)(2,1)S(1)}, bf16[8,64,256]{2,1,0:T(8,128)(2,1)}, u32[]{:S(2)}, u32[]{:S(2)}) collective-permute-start(bf16[8,64,256]{2,1,0:T(8,128)(2,1)S(1)} %collective-permute-done.1.refs_4_), channel_id=1, source_target_pairs={{0,16},{16,0},{1,17},{17,1},{2,18},{18,2},{3,19},{19,3},{4,20},{20... | collective-permute-start | bytes 786440 | tf_op jit(solution)/shard_map/ppermute | solution.py:55
  47.3 2.2 %collective-permute-start.14 = (bf16[8,64,256]{2,1,0:T(8,128)(2,1)S(1)}, bf16[8,64,256]{2,1,0:T(8,128)(2,1)}, u32[]{:S(2)}, u32[]{:S(2)}) collective-permute-start(bf16[8,64,256]{2,1,0:T(8,128)(2,1)S(1)} %collective-permute-done.6.refs_7_), channel_id=1, source_target_pairs={{0,16},{16,0},{1,17},{17,1},{2,18},{18,2},{3,19},{19,3},{4,20},{20... | collective-permute-start | bytes 786440 | tf_op jit(solution)/shard_map/ppermute | solution.py:55
  47.8 1.9 %collective-permute-start.13 = (bf16[8,64,256]{2,1,0:T(8,128)(2,1)S(1)}, bf16[8,64,256]{2,1,0:T(8,128)(2,1)}, u32[]{:S(2)}, u32[]{:S(2)}) collective-permute-start(bf16[8,64,256]{2,1,0:T(8,128)(2,1)S(1)} %collective-permute-done.5.refs_6_), channel_id=1, source_target_pairs={{0,16},{16,0},{1,17},{17,1},{2,18},{18,2},{3,19},{19,3},{4,20},{20... | collective-permute-start | bytes 786440 | tf_op jit(solution)/shard_map/ppermute | solution.py:55
  48.5 1.7 %collective-permute-start.12 = (bf16[8,64,256]{2,1,0:T(8,128)(2,1)S(1)}, bf16[8,64,256]{2,1,0:T(8,128)(2,1)}, u32[]{:S(2)}, u32[]{:S(2)}) collective-permute-start(bf16[8,64,256]{2,1,0:T(8,128)(2,1)S(1)} %collective-permute-done.4.refs_5_), channel_id=1, source_target_pairs={{0,16},{16,0},{1,17},{17,1},{2,18},{18,2},{3,19},{19,3},{4,20},{20... | collective-permute-start | bytes 786440 | tf_op jit(solution)/shard_map/ppermute | solution.py:55
  65.2 2.7 %collective-permute-start.15 = (bf16[4,8,64,256]{3,2,1,0:T(8,128)(2,1)S(1)}, bf16[4,8,64,256]{3,2,1,0:T(8,128)(2,1)S(1)}, u32[]{:S(2)}, u32[]{:S(2)}) collective-permute-start(bf16[4,8,64,256]{3,2,1,0:T(8,128)(2,1)S(1)} %get-tuple-element.43), channel_id=1, source_target_pairs={{0,16},{16,0},{1,17},{17,1},{2,18},{18,2},{3,19},{19,3},{4,20},{20... | collective-permute-start | bytes 3145736 | tf_op jit(solution)/shard_map/ppermute | solution.py:55
  65.4 7.5 %collective-permute-start.16 = (bf16[4,8,64,256]{3,2,1,0:T(8,128)(2,1)S(1)}, bf16[4,8,64,256]{3,2,1,0:T(8,128)(2,1)S(1)}, u32[]{:S(2)}, u32[]{:S(2)}) collective-permute-start(bf16[4,8,64,256]{3,2,1,0:T(8,128)(2,1)S(1)} %get-tuple-element.49), channel_id=1, source_target_pairs={{0,16},{16,0},{1,17},{17,1},{2,18},{18,2},{3,19},{19,3},{4,20},{20... | collective-permute-start | bytes 3145736 | tf_op jit(solution)/shard_map/ppermute | solution.py:55
  68.2 6.8 %collective-permute-start.20 = (bf16[8,64,256]{2,1,0:T(8,128)(2,1)S(1)}, bf16[8,64,256]{2,1,0:T(8,128)(2,1)S(1)}, u32[]{:S(2)}, u32[]{:S(2)}) collective-permute-start(bf16[8,64,256]{2,1,0:T(8,128)(2,1)S(1)} %get-tuple-element.55), channel_id=1, source_target_pairs={{0,4},{2,6},{4,8},{6,10},{8,12},{10,14},{12,0},{14,2},{16,48},{18,... | collective-permute-start | bytes 786440 | tf_op jit(solution)/shard_map/ppermute | solution.py:43
  68.3 12.7 %collective-permute-start.21 = (bf16[8,64,256]{2,1,0:T(8,128)(2,1)S(1)}, bf16[8,64,256]{2,1,0:T(8,128)(2,1)S(1)}, u32[]{:S(2)}, u32[]{:S(2)}) collective-permute-start(bf16[8,64,256]{2,1,0:T(8,128)(2,1)S(1)} %get-tuple-element.56), channel_id=1, source_target_pairs={{0,8},{2,10},{4,12},{6,14},{8,0},{10,2},{12,4},{14,6},{16,80},{18,... | collective-permute-start | bytes 786440 | tf_op jit(solution)/shard_map/ppermute | solution.py:43
  68.5 12.6 %collective-permute-start.22 = (bf16[8,64,256]{2,1,0:T(8,128)(2,1)S(1)}, bf16[8,64,256]{2,1,0:T(8,128)(2,1)S(1)}, u32[]{:S(2)}, u32[]{:S(2)}) collective-permute-start(bf16[8,64,256]{2,1,0:T(8,128)(2,1)S(1)} %get-tuple-element.57), channel_id=1, source_target_pairs={{0,12},{2,14},{4,0},{6,2},{8,4},{10,6},{12,8},{14,10},{16,240},{18... | collective-permute-start | bytes 786440 | tf_op jit(solution)/shard_map/ppermute | solution.py:43
  73.1 10.3 %collective-permute-start.17 = (bf16[8,64,256]{2,1,0:T(8,128)(2,1)S(1)}, bf16[8,64,256]{2,1,0:T(8,128)(2,1)S(1)}, u32[]{:S(2)}, u32[]{:S(2)}) collective-permute-start(bf16[8,64,256]{2,1,0:T(8,128)(2,1)S(1)} %get-tuple-element.51), channel_id=1, source_target_pairs={{0,4},{2,6},{4,8},{6,10},{8,12},{10,14},{12,0},{14,2},{16,48},{18,... | collective-permute-start | bytes 786440 | tf_op jit(solution)/shard_map/ppermute | solution.py:43
  73.2 16.1 %collective-permute-start.18 = (bf16[8,64,256]{2,1,0:T(8,128)(2,1)S(1)}, bf16[8,64,256]{2,1,0:T(8,128)(2,1)S(1)}, u32[]{:S(2)}, u32[]{:S(2)}) collective-permute-start(bf16[8,64,256]{2,1,0:T(8,128)(2,1)S(1)} %get-tuple-element.52), channel_id=1, source_target_pairs={{0,8},{2,10},{4,12},{6,14},{8,0},{10,2},{12,4},{14,6},{16,80},{18,... | collective-permute-start | bytes 786440 | tf_op jit(solution)/shard_map/ppermute | solution.py:43
  75.0 14.3 %collective-permute-start.19 = (bf16[8,64,256]{2,1,0:T(8,128)(2,1)S(1)}, bf16[8,64,256]{2,1,0:T(8,128)(2,1)S(1)}, u32[]{:S(2)}, u32[]{:S(2)}) collective-permute-start(bf16[8,64,256]{2,1,0:T(8,128)(2,1)S(1)} %get-tuple-element.53), channel_id=1, source_target_pairs={{0,12},{2,14},{4,0},{6,2},{8,4},{10,6},{12,8},{14,10},{16,240},{18... | collective-permute-start | bytes 786440 | tf_op jit(solution)/shard_map/ppermute | solution.py:43
  81.2 13.0 %collective-permute-start.23 = (bf16[8,64,256]{2,1,0:T(8,128)(2,1)S(1)}, bf16[8,64,256]{2,1,0:T(8,128)(2,1)S(1)}, u32[]{:S(2)}, u32[]{:S(2)}) collective-permute-start(bf16[8,64,256]{2,1,0:T(8,128)(2,1)S(1)} %add_convert_fusion.1), channel_id=1, source_target_pairs={{0,2},{2,0},{4,6},{6,4},{8,10},{10,8},{12,14},{14,12},{16,144},{18... | collective-permute-start | bytes 786440 | tf_op jit(solution)/shard_map/ppermute | solution.py:43
  (8 other events, 217.1 us)

commit v3 on v2

--- a/solution.py
+++ b/solution.py
@@ -289,12 +289,13 @@
     near = small_stage(jnp.broadcast_to(enc_out, (NB, TB, FB)))
     far = across(near)
     own = [near] + [big_stage(near, i, -1) for i in (1, 2, 3)]
-    own[1], far, kv_weight = lax.optimization_barrier((own[1], far, kv_weight))
+    first = twin(near)
+    first, own[1], far, kv_weight = lax.optimization_barrier((first, own[1], far, kv_weight))
     weight, mark = relayout(pltpu.with_memory_space_constraint(kv_weight, pltpu.HBM))
     held = pltpu.with_memory_space_constraint(weight, pltpu.HBM)
     own += [far] + [big_stage(far, i, -1) for i in (1, 2, 3)]
-    *own[:5], mark = lax.optimization_barrier((*own[:5], mark))
-    other = [pltpu.with_memory_space_constraint(twin(v), pltpu.HBM) for v in own]
+    *own[1:5], mark = lax.optimization_barrier((*own[1:5], mark))
+    other = [pltpu.with_memory_space_constraint(v, pltpu.HBM) for v in [first] + [twin(v) for v in own[1:]]]
 
     enc_col = enc_seg.reshape(NB * TB, 1)
     context, grads, home, away = main(place, own, other, held, mark, dec_query[0, 0], ctx_grad[0, 0], enc_col, dec_seg)

time: 106 us -> 105 us (level)
  starting transfers between devices: 18.9 us -> 22.9 us
  waiting for transfers between devices: 30.9 us -> 27.5 us
    ppermute x10, starting transfers between devices: 3.12 us -> 8.58 us  [twin(): return lax.ppermute(value, 'c', [(0, 1), (1, 0)])]
    ppermute x14, waiting for transfers between devices: 30.1 us -> 26.5 us  [joint(): return lax.ppermute(value, AXES, pairs)]
    ppermute x14, starting transfers between devices: 15.8 us -> 14.3 us  [joint(): return lax.ppermute(value, AXES, pairs)]
  transfers between devices with their start and end apart: 24 -> 24, of which waited for: 11 -> 10; matrix products, arithmetic and copies ran while one was open for 0% -> 0% of each run, Pallas kernels for 11% -> 11%
where the time goes in v3:
time: 105 us
  waiting for transfers between devices  27.5 us (26%)
  Pallas kernels  26.4 us (25%)
  blocking collectives  24.9 us (24%)
  starting transfers between devices  22.9 us (22%)
  local copies, waits for them, and re-layouts  1.43 us (1%)
  other arithmetic  1.08 us (1%)
    ppermute x14, waiting for transfers between devices, joint(): return lax.ppermute(value, AXES, pairs)  26.5 us
    all_to_all x2, blocking collectives, small_stage(): return lax.all_to_all(value, AXES, 0, 0, axis_index_groups=SMALL_GROUPS)  24.9 us
    pallas_call x1, Pallas kernels, main(): pl.pallas_call(main_kernel, in_specs=[SMEM] + whole(16) + [HBM] + whole(5...  14.9 us
    ppermute x14, starting transfers between devices, joint(): return lax.ppermute(value, AXES, pairs)  14.3 us
    ppermute x10, starting transfers between devices, twin(): return lax.ppermute(value, 'c', [(0, 1), (1, 0)])  8.58 us
    pallas_call x1, Pallas kernels, relayout(): pl.pallas_call(relayout_kernel, in_specs=[HBM], out_specs=[HBM] + whole(1...  7.17 us
    pallas_call x2, Pallas kernels, spread_own(): pl.pallas_call(functools.partial(plain_kernel, b), in_specs=[SMEM] + whol...  3.91 us
  transfers between devices with their start and end apart: 24, of which 10 were waited for; matrix products, arithmetic and copies ran while one was open for 0% of the time, Pallas kernels for 11%

profile of v3, /device:TPU:1, one launch (start us, length us, event | category | flops | bytes accessed | tf_op | source)
XLA Modules:
  0.0 105.0 jit_solution(3179598579445992800)
XLA Ops:
  0.7 0.9 broadcast_in_dim.14
  1.5 14.6 %all_to_all.10.refs_0_ = bf16[8,64,256]{2,1,0:T(8,128)(2,1)S(1)} all-to-all(bf16[8,64,256]{2,1,0:T(8,128)(2,1)S(1)} %broadcast_in_dim.14), channel_id=1, replica_groups={{0,32,64,96,128,160,192,224},{2,34,66,98,130,162,194,226},{4,36,68,100,..., dimensions={0} | all-to-all | bytes 524288 | tf_op jit(solution)/shard_map/all_to_all | solution.py:32
  16.1 6.9 %collective-permute-start.2 = (bf16[8,64,256]{2,1,0:T(8,128)(2,1)S(1)}, bf16[8,64,256]{2,1,0:T(8,128)(2,1)S(1)}, u32[]{:S(2)}, u32[]{:S(2)}) collective-permute-start(bf16[8,64,256]{2,1,0:T(8,128)(2,1)S(1)} %all_to_all.10.refs_0_), channel_id=1, source_target_pairs={{0,2},{2,0},{4,6},{6,4},{8,10},{10,8},{12,14},{14,12},{16,144},{18... | collective-permute-start | bytes 786440 | tf_op jit(solution)/shard_map/ppermute | solution.py:43
  23.0 5.1 %collective-permute-start = (bf16[8,64,256]{2,1,0:T(8,128)(2,1)S(1)}, bf16[8,64,256]{2,1,0:T(8,128)(2,1)S(1)}, u32[]{:S(2)}, u32[]{:S(2)}) collective-permute-start(bf16[8,64,256]{2,1,0:T(8,128)(2,1)S(1)} %all_to_all.10.refs_0_), channel_id=1, source_target_pairs={{0,16},{16,0},{1,17},{17,1},{2,18},{18,2},{3,19},{19,3},{4,20},{20... | collective-permute-start | bytes 786440 | tf_op jit(solution)/shard_map/ppermute | solution.py:55
  28.1 5.5 %collective-permute-done.1.refs_1_ = bf16[8,64,256]{2,1,0:T(8,128)(2,1)S(1)} collective-permute-done((bf16[8,64,256]{2,1,0:T(8,128)(2,1)S(1)}, bf16[8,64,256]{2,1,0:T(8,128)(2,1)S(1)}, u32[]{:S(2)}, u32[]{:S(2)}) %collective-permute-start.1) | collective-permute-done | bytes 262176 | tf_op jit(solution)/shard_map/ppermute | solution.py:43
  33.6 2.9 %collective-permute-start.6 = (bf16[8,64,256]{2,1,0:T(8,128)(2,1)S(1)}, bf16[8,64,256]{2,1,0:T(8,128)(2,1)S(1)}, u32[]{:S(2)}, u32[]{:S(2)}) collective-permute-start(bf16[8,64,256]{2,1,0:T(8,128)(2,1)S(1)} %collective-permute-done.2.refs_4_), channel_id=1, source_target_pairs={{0,8},{2,10},{4,12},{6,14},{8,0},{10,2},{12,4},{14,6},{16,208},{18... | collective-permute-start | bytes 786440 | tf_op jit(solution)/shard_map/ppermute | solution.py:43
  36.6 7.2 %relayout.1 = (bf16[8,2,256,1024]{3,2,1,0:T(8,128)(2,1)}, f32[8,128]{1,0:T(8,128)S(1)}) custom-call(bf16[1,4096,2,512]{3,2,1,0:T(2,128)(2,1)} %w_ref), custom_call_target="tpu_custom_call" | custom-call | tf_op jit(solution)/shard_map/relayout/pallas_call | solution.py:87
  43.8 1.2 %collective-permute-start.8 = (bf16[8,64,256]{2,1,0:T(8,128)(2,1)S(1)}, bf16[8,64,256]{2,1,0:T(8,128)(2,1)S(1)}, u32[]{:S(2)}, u32[]{:S(2)}) collective-permute-start(bf16[8,64,256]{2,1,0:T(8,128)(2,1)S(1)} %collective-permute-done.1.refs_1_), channel_id=1, source_target_pairs={{0,16},{16,0},{1,17},{17,1},{2,18},{18,2},{3,19},{19,3},{4,20},{20... | collective-permute-start | bytes 786440 | tf_op jit(solution)/shard_map/ppermute | solution.py:55
  45.5 1.8 %collective-permute-done.5.refs_5_ = bf16[8,64,256]{2,1,0:T(8,128)(2,1)S(1)} collective-permute-done((bf16[8,64,256]{2,1,0:T(8,128)(2,1)S(1)}, bf16[8,64,256]{2,1,0:T(8,128)(2,1)S(1)}, u32[]{:S(2)}, u32[]{:S(2)}) %collective-permute-start.5) | collective-permute-done | bytes 262176 | tf_op jit(solution)/shard_map/ppermute | solution.py:43
  47.3 0.5 collective-permute-start.13
  48.0 0.5 collective-permute-start.12
  49.8 14.9 %main.1 = (bf16[512,512]{1,0:T(8,128)(2,1)}, bf16[512,1024]{1,0:T(8,128)(2,1)S(1)}, bf16[4,8,64,256]{3,2,1,0:T(8,128)(2,1)S(1)}, bf16[4,8,64,256]{3,2,1,0:T(8,128)(2,1)S(1)}) custom-call(s32[4]{0:T(128)S(1)} %pad_add_fusion.place_ref, bf16[8,64,256]{2,1,0:T(8,128)(2,1)S(1)} %all_to_all.10.refs_0_, bf16[8,64,256]{2,1,0:T(8,128)(2,1)S(1)} %collective-permute-done.1.refs_1_, ...), custom_call_target="tpu_custom_call" | custom-call | tf_op jit(solution)/shard_map/main/pallas_call | solution.py:201
  64.7 0.6 collective-permute-start.15
  65.4 2.1 %spread_own.2.one_ref = bf16[4,8,64,256]{3,2,1,0:T(8,128)(2,1)S(1)} custom-call(s32[4]{0:T(128)S(1)} %pad_add_fusion.place_ref, bf16[512,1024]{1,0:T(8,128)(2,1)S(1)} %get-tuple-element.48.grad_ref, bf16[8,2,256,1024]{3,2,1,0:T(8,128)(2,1)S(1)} %copy-done), custom_call_target="tpu_custom_call" | custom-call | tf_op jit(solution)/shard_map/spread_own/pallas_call | solution.py:254
  68.1 2.6 %collective-permute-start.22 = (bf16[8,64,256]{2,1,0:T(8,128)(2,1)S(1)}, bf16[8,64,256]{2,1,0:T(8,128)(2,1)S(1)}, u32[]{:S(2)}, u32[]{:S(2)}) collective-permute-start(bf16[8,64,256]{2,1,0:T(8,128)(2,1)S(1)} %get-tuple-element.57), channel_id=1, source_target_pairs={{0,12},{2,14},{4,0},{6,2},{8,4},{10,6},{12,8},{14,10},{16,240},{18... | collective-permute-start | bytes 786440 | tf_op jit(solution)/shard_map/ppermute | solution.py:43
  70.6 1.8 %spread_own.3.one_ref = bf16[4,8,64,256]{3,2,1,0:T(8,128)(2,1)S(1)} custom-call(s32[4]{0:T(128)S(1)} %pad_add_fusion.place_ref, bf16[512,1024]{1,0:T(8,128)(2,1)S(1)} %get-tuple-element.48.grad_ref, bf16[8,2,256,1024]{3,2,1,0:T(8,128)(2,1)S(1)} %copy-done), custom_call_target="tpu_custom_call" | custom-call | tf_op jit(solution)/shard_map/spread_own/pallas_call | solution.py:254
  73.2 1.4 %collective-permute-done.20 = bf16[8,64,256]{2,1,0:T(8,128)(2,1)S(1)} collective-permute-done((bf16[8,64,256]{2,1,0:T(8,128)(2,1)S(1)}, bf16[8,64,256]{2,1,0:T(8,128)(2,1)S(1)}, u32[]{:S(2)}, u32[]{:S(2)}) %collective-permute-start.20) | collective-permute-done | bytes 262176 | tf_op jit(solution)/shard_map/ppermute | solution.py:43
  74.6 1.1 %collective-permute-start.19 = (bf16[8,64,256]{2,1,0:T(8,128)(2,1)S(1)}, bf16[8,64,256]{2,1,0:T(8,128)(2,1)S(1)}, u32[]{:S(2)}, u32[]{:S(2)}) collective-permute-start(bf16[8,64,256]{2,1,0:T(8,128)(2,1)S(1)} %get-tuple-element.53), channel_id=1, source_target_pairs={{0,12},{2,14},{4,0},{6,2},{8,4},{10,6},{12,8},{14,10},{16,240},{18... | collective-permute-start | bytes 786440 | tf_op jit(solution)/shard_map/ppermute | solution.py:43
  75.7 5.0 %collective-permute-done.21 = bf16[8,64,256]{2,1,0:T(8,128)(2,1)S(1)} collective-permute-done((bf16[8,64,256]{2,1,0:T(8,128)(2,1)S(1)}, bf16[8,64,256]{2,1,0:T(8,128)(2,1)S(1)}, u32[]{:S(2)}, u32[]{:S(2)}) %collective-permute-start.21) | collective-permute-done | bytes 262176 | tf_op jit(solution)/shard_map/ppermute | solution.py:43
  80.9 2.1 %collective-permute-done.17 = bf16[8,64,256]{2,1,0:T(8,128)(2,1)S(1)} collective-permute-done((bf16[8,64,256]{2,1,0:T(8,128)(2,1)S(1)}, bf16[8,64,256]{2,1,0:T(8,128)(2,1)S(1)}, u32[]{:S(2)}, u32[]{:S(2)}) %collective-permute-start.17) | collective-permute-done | bytes 262176 | tf_op jit(solution)/shard_map/ppermute | solution.py:43
  83.0 5.9 %collective-permute-done.18 = bf16[8,64,256]{2,1,0:T(8,128)(2,1)S(1)} collective-permute-done((bf16[8,64,256]{2,1,0:T(8,128)(2,1)S(1)}, bf16[8,64,256]{2,1,0:T(8,128)(2,1)S(1)}, u32[]{:S(2)}, u32[]{:S(2)}) %collective-permute-start.18) | collective-permute-done | bytes 262176 | tf_op jit(solution)/shard_map/ppermute | solution.py:43
  89.0 4.8 %collective-permute-done.23 = bf16[8,64,256]{2,1,0:T(8,128)(2,1)S(1)} collective-permute-done((bf16[8,64,256]{2,1,0:T(8,128)(2,1)S(1)}, bf16[8,64,256]{2,1,0:T(8,128)(2,1)S(1)}, u32[]{:S(2)}, u32[]{:S(2)}) %collective-permute-start.23) | collective-permute-done | bytes 262176 | tf_op jit(solution)/shard_map/ppermute | solution.py:43
  94.0 10.3 %all_to_all.11 = bf16[8,64,256]{2,1,0:T(8,128)(2,1)S(1)} all-to-all(bf16[8,64,256]{2,1,0:T(8,128)(2,1)S(1)} %add_convert_fusion), channel_id=1, replica_groups={{0,32,64,96,128,160,192,224},{2,34,66,98,130,162,194,226},{4,36,68,100,..., dimensions={0} | all-to-all | bytes 524288 | tf_op jit(solution)/shard_map/all_to_all | solution.py:32
  104.3 0.7 convert_reduce_fusion
  (54 shorter events, 4.0 us)
Async XLA Ops:
  16.1 12.0 %collective-permute-start.2 = (bf16[8,64,256]{2,1,0:T(8,128)(2,1)S(1)}, bf16[8,64,256]{2,1,0:T(8,128)(2,1)S(1)}, u32[]{:S(2)}, u32[]{:S(2)}) collective-permute-start(bf16[8,64,256]{2,1,0:T(8,128)(2,1)S(1)} %all_to_all.10.refs_0_), channel_id=1, source_target_pairs={{0,2},{2,0},{4,6},{6,4},{8,10},{10,8},{12,14},{14,12},{16,144},{18... | collective-permute-start | bytes 786440 | tf_op jit(solution)/shard_map/ppermute | solution.py:43
  23.0 10.6 %collective-permute-start.1 = (bf16[8,64,256]{2,1,0:T(8,128)(2,1)S(1)}, bf16[8,64,256]{2,1,0:T(8,128)(2,1)S(1)}, u32[]{:S(2)}, u32[]{:S(2)}) collective-permute-start(bf16[8,64,256]{2,1,0:T(8,128)(2,1)S(1)} %all_to_all.10.refs_0_), channel_id=1, source_target_pairs={{0,12},{2,14},{4,0},{6,2},{8,4},{10,6},{12,8},{14,10},{16,240},{18... | collective-permute-start | bytes 786440 | tf_op jit(solution)/shard_map/ppermute | solution.py:43
  23.0 10.6 %collective-permute-start = (bf16[8,64,256]{2,1,0:T(8,128)(2,1)S(1)}, bf16[8,64,256]{2,1,0:T(8,128)(2,1)S(1)}, u32[]{:S(2)}, u32[]{:S(2)}) collective-permute-start(bf16[8,64,256]{2,1,0:T(8,128)(2,1)S(1)} %all_to_all.10.refs_0_), channel_id=1, source_target_pairs={{0,16},{16,0},{1,17},{17,1},{2,18},{18,2},{3,19},{19,3},{4,20},{20... | collective-permute-start | bytes 786440 | tf_op jit(solution)/shard_map/ppermute | solution.py:55
  28.1 15.6 %collective-permute-start.4 = (bf16[8,64,256]{2,1,0:T(8,128)(2,1)S(1)}, bf16[8,64,256]{2,1,0:T(8,128)(2,1)S(1)}, u32[]{:S(2)}, u32[]{:S(2)}) collective-permute-start(bf16[8,64,256]{2,1,0:T(8,128)(2,1)S(1)} %all_to_all.10.refs_0_), channel_id=1, source_target_pairs={{0,4},{2,6},{4,8},{6,10},{8,12},{10,14},{12,0},{14,2},{16,48},{18,... | collective-permute-start | bytes 786440 | tf_op jit(solution)/shard_map/ppermute | solution.py:43
  28.1 15.6 %collective-permute-start.3 = (bf16[8,64,256]{2,1,0:T(8,128)(2,1)S(1)}, bf16[8,64,256]{2,1,0:T(8,128)(2,1)S(1)}, u32[]{:S(2)}, u32[]{:S(2)}) collective-permute-start(bf16[8,64,256]{2,1,0:T(8,128)(2,1)S(1)} %all_to_all.10.refs_0_), channel_id=1, source_target_pairs={{0,8},{2,10},{4,12},{6,14},{8,0},{10,2},{12,4},{14,6},{16,208},{18... | collective-permute-start | bytes 786440 | tf_op jit(solution)/shard_map/ppermute | solution.py:43
  33.6 11.4 %collective-permute-start.7 = (bf16[8,64,256]{2,1,0:T(8,128)(2,1)S(1)}, bf16[8,64,256]{2,1,0:T(8,128)(2,1)S(1)}, u32[]{:S(2)}, u32[]{:S(2)}) collective-permute-start(bf16[8,64,256]{2,1,0:T(8,128)(2,1)S(1)} %collective-permute-done.2.refs_4_), channel_id=1, source_target_pairs={{0,4},{2,6},{4,8},{6,10},{8,12},{10,14},{12,0},{14,2},{16,48},{18,... | collective-permute-start | bytes 786440 | tf_op jit(solution)/shard_map/ppermute | solution.py:43
  33.6 11.8 %collective-permute-start.6 = (bf16[8,64,256]{2,1,0:T(8,128)(2,1)S(1)}, bf16[8,64,256]{2,1,0:T(8,128)(2,1)S(1)}, u32[]{:S(2)}, u32[]{:S(2)}) collective-permute-start(bf16[8,64,256]{2,1,0:T(8,128)(2,1)S(1)} %collective-permute-done.2.refs_4_), channel_id=1, source_target_pairs={{0,8},{2,10},{4,12},{6,14},{8,0},{10,2},{12,4},{14,6},{16,208},{18... | collective-permute-start | bytes 786440 | tf_op jit(solution)/shard_map/ppermute | solution.py:43
  36.6 10.8 %collective-permute-start.5 = (bf16[8,64,256]{2,1,0:T(8,128)(2,1)S(1)}, bf16[8,64,256]{2,1,0:T(8,128)(2,1)S(1)}, u32[]{:S(2)}, u32[]{:S(2)}) collective-permute-start(bf16[8,64,256]{2,1,0:T(8,128)(2,1)S(1)} %collective-permute-done.2.refs_4_), channel_id=1, source_target_pairs={{0,12},{2,14},{4,0},{6,2},{8,4},{10,6},{12,8},{14,10},{16,240},{18... | collective-permute-start | bytes 786440 | tf_op jit(solution)/shard_map/ppermute | solution.py:43
  43.8 3.6 %collective-permute-start.8 = (bf16[8,64,256]{2,1,0:T(8,128)(2,1)S(1)}, bf16[8,64,256]{2,1,0:T(8,128)(2,1)S(1)}, u32[]{:S(2)}, u32[]{:S(2)}) collective-permute-start(bf16[8,64,256]{2,1,0:T(8,128)(2,1)S(1)} %collective-permute-done.1.refs_1_), channel_id=1, source_target_pairs={{0,16},{16,0},{1,17},{17,1},{2,18},{18,2},{3,19},{19,3},{4,20},{20... | collective-permute-start | bytes 786440 | tf_op jit(solution)/shard_map/ppermute | solution.py:55
  44.9 2.9 %collective-permute-start.9 = (bf16[8,64,256]{2,1,0:T(8,128)(2,1)S(1)}, bf16[8,64,256]{2,1,0:T(8,128)(2,1)S(1)}, u32[]{:S(2)}, u32[]{:S(2)}) collective-permute-start(bf16[8,64,256]{2,1,0:T(8,128)(2,1)S(1)} %collective-permute-done.3.refs_2_), channel_id=1, source_target_pairs={{0,16},{16,0},{1,17},{17,1},{2,18},{18,2},{3,19},{19,3},{4,20},{20... | collective-permute-start | bytes 786440 | tf_op jit(solution)/shard_map/ppermute | solution.py:55
  45.0 4.0 %collective-permute-start.10 = (bf16[8,64,256]{2,1,0:T(8,128)(2,1)S(1)}, bf16[8,64,256]{2,1,0:T(8,128)(2,1)}, u32[]{:S(2)}, u32[]{:S(2)}) collective-permute-start(bf16[8,64,256]{2,1,0:T(8,128)(2,1)S(1)} %collective-permute-done.4.refs_3_), channel_id=1, source_target_pairs={{0,16},{16,0},{1,17},{17,1},{2,18},{18,2},{3,19},{19,3},{4,20},{20... | collective-permute-start | bytes 786440 | tf_op jit(solution)/shard_map/ppermute | solution.py:55
  45.4 3.5 %collective-permute-start.11 = (bf16[8,64,256]{2,1,0:T(8,128)(2,1)S(1)}, bf16[8,64,256]{2,1,0:T(8,128)(2,1)}, u32[]{:S(2)}, u32[]{:S(2)}) collective-permute-start(bf16[8,64,256]{2,1,0:T(8,128)(2,1)S(1)} %collective-permute-done.2.refs_4_), channel_id=1, source_target_pairs={{0,16},{16,0},{1,17},{17,1},{2,18},{18,2},{3,19},{19,3},{4,20},{20... | collective-permute-start | bytes 786440 | tf_op jit(solution)/shard_map/ppermute | solution.py:55
  47.3 1.7 %collective-permute-start.14 = (bf16[8,64,256]{2,1,0:T(8,128)(2,1)S(1)}, bf16[8,64,256]{2,1,0:T(8,128)(2,1)}, u32[]{:S(2)}, u32[]{:S(2)}) collective-permute-start(bf16[8,64,256]{2,1,0:T(8,128)(2,1)S(1)} %collective-permute-done.7.refs_7_), channel_id=1, source_target_pairs={{0,16},{16,0},{1,17},{17,1},{2,18},{18,2},{3,19},{19,3},{4,20},{20... | collective-permute-start | bytes 786440 | tf_op jit(solution)/shard_map/ppermute | solution.py:55
  47.3 2.0 %collective-permute-start.13 = (bf16[8,64,256]{2,1,0:T(8,128)(2,1)S(1)}, bf16[8,64,256]{2,1,0:T(8,128)(2,1)}, u32[]{:S(2)}, u32[]{:S(2)}) collective-permute-start(bf16[8,64,256]{2,1,0:T(8,128)(2,1)S(1)} %collective-permute-done.6.refs_6_), channel_id=1, source_target_pairs={{0,16},{16,0},{1,17},{17,1},{2,18},{18,2},{3,19},{19,3},{4,20},{20... | collective-permute-start | bytes 786440 | tf_op jit(solution)/shard_map/ppermute | solution.py:55
  48.0 1.8 %collective-permute-start.12 = (bf16[8,64,256]{2,1,0:T(8,128)(2,1)S(1)}, bf16[8,64,256]{2,1,0:T(8,128)(2,1)}, u32[]{:S(2)}, u32[]{:S(2)}) collective-permute-start(bf16[8,64,256]{2,1,0:T(8,128)(2,1)S(1)} %collective-permute-done.5.refs_5_), channel_id=1, source_target_pairs={{0,16},{16,0},{1,17},{17,1},{2,18},{18,2},{3,19},{19,3},{4,20},{20... | collective-permute-start | bytes 786440 | tf_op jit(solution)/shard_map/ppermute | solution.py:55
  64.7 2.9 %collective-permute-start.15 = (bf16[4,8,64,256]{3,2,1,0:T(8,128)(2,1)S(1)}, bf16[4,8,64,256]{3,2,1,0:T(8,128)(2,1)S(1)}, u32[]{:S(2)}, u32[]{:S(2)}) collective-permute-start(bf16[4,8,64,256]{3,2,1,0:T(8,128)(2,1)S(1)} %get-tuple-element.43), channel_id=1, source_target_pairs={{0,16},{16,0},{1,17},{17,1},{2,18},{18,2},{3,19},{19,3},{4,20},{20... | collective-permute-start | bytes 3145736 | tf_op jit(solution)/shard_map/ppermute | solution.py:55
  65.3 7.2 %collective-permute-start.16 = (bf16[4,8,64,256]{3,2,1,0:T(8,128)(2,1)S(1)}, bf16[4,8,64,256]{3,2,1,0:T(8,128)(2,1)S(1)}, u32[]{:S(2)}, u32[]{:S(2)}) collective-permute-start(bf16[4,8,64,256]{3,2,1,0:T(8,128)(2,1)S(1)} %get-tuple-element.49), channel_id=1, source_target_pairs={{0,16},{16,0},{1,17},{17,1},{2,18},{18,2},{3,19},{19,3},{4,20},{20... | collective-permute-start | bytes 3145736 | tf_op jit(solution)/shard_map/ppermute | solution.py:55
  67.8 6.8 %collective-permute-start.20 = (bf16[8,64,256]{2,1,0:T(8,128)(2,1)S(1)}, bf16[8,64,256]{2,1,0:T(8,128)(2,1)S(1)}, u32[]{:S(2)}, u32[]{:S(2)}) collective-permute-start(bf16[8,64,256]{2,1,0:T(8,128)(2,1)S(1)} %get-tuple-element.55), channel_id=1, source_target_pairs={{0,4},{2,6},{4,8},{6,10},{8,12},{10,14},{12,0},{14,2},{16,48},{18,... | collective-permute-start | bytes 786440 | tf_op jit(solution)/shard_map/ppermute | solution.py:43
  67.9 12.8 %collective-permute-start.21 = (bf16[8,64,256]{2,1,0:T(8,128)(2,1)S(1)}, bf16[8,64,256]{2,1,0:T(8,128)(2,1)S(1)}, u32[]{:S(2)}, u32[]{:S(2)}) collective-permute-start(bf16[8,64,256]{2,1,0:T(8,128)(2,1)S(1)} %get-tuple-element.56), channel_id=1, source_target_pairs={{0,8},{2,10},{4,12},{6,14},{8,0},{10,2},{12,4},{14,6},{16,80},{18,... | collective-permute-start | bytes 786440 | tf_op jit(solution)/shard_map/ppermute | solution.py:43
  68.1 12.6 %collective-permute-start.22 = (bf16[8,64,256]{2,1,0:T(8,128)(2,1)S(1)}, bf16[8,64,256]{2,1,0:T(8,128)(2,1)S(1)}, u32[]{:S(2)}, u32[]{:S(2)}) collective-permute-start(bf16[8,64,256]{2,1,0:T(8,128)(2,1)S(1)} %get-tuple-element.57), channel_id=1, source_target_pairs={{0,12},{2,14},{4,0},{6,2},{8,4},{10,6},{12,8},{14,10},{16,240},{18... | collective-permute-start | bytes 786440 | tf_op jit(solution)/shard_map/ppermute | solution.py:43
  72.7 10.3 %collective-permute-start.17 = (bf16[8,64,256]{2,1,0:T(8,128)(2,1)S(1)}, bf16[8,64,256]{2,1,0:T(8,128)(2,1)S(1)}, u32[]{:S(2)}, u32[]{:S(2)}) collective-permute-start(bf16[8,64,256]{2,1,0:T(8,128)(2,1)S(1)} %get-tuple-element.51), channel_id=1, source_target_pairs={{0,4},{2,6},{4,8},{6,10},{8,12},{10,14},{12,0},{14,2},{16,48},{18,... | collective-permute-start | bytes 786440 | tf_op jit(solution)/shard_map/ppermute | solution.py:43
  72.8 16.1 %collective-permute-start.18 = (bf16[8,64,256]{2,1,0:T(8,128)(2,1)S(1)}, bf16[8,64,256]{2,1,0:T(8,128)(2,1)S(1)}, u32[]{:S(2)}, u32[]{:S(2)}) collective-permute-start(bf16[8,64,256]{2,1,0:T(8,128)(2,1)S(1)} %get-tuple-element.52), channel_id=1, source_target_pairs={{0,8},{2,10},{4,12},{6,14},{8,0},{10,2},{12,4},{14,6},{16,80},{18,... | collective-permute-start | bytes 786440 | tf_op jit(solution)/shard_map/ppermute | solution.py:43
  74.6 14.3 %collective-permute-start.19 = (bf16[8,64,256]{2,1,0:T(8,128)(2,1)S(1)}, bf16[8,64,256]{2,1,0:T(8,128)(2,1)S(1)}, u32[]{:S(2)}, u32[]{:S(2)}) collective-permute-start(bf16[8,64,256]{2,1,0:T(8,128)(2,1)S(1)} %get-tuple-element.53), channel_id=1, source_target_pairs={{0,12},{2,14},{4,0},{6,2},{8,4},{10,6},{12,8},{14,10},{16,240},{18... | collective-permute-start | bytes 786440 | tf_op jit(solution)/shard_map/ppermute | solution.py:43
  80.8 13.0 %collective-permute-start.23 = (bf16[8,64,256]{2,1,0:T(8,128)(2,1)S(1)}, bf16[8,64,256]{2,1,0:T(8,128)(2,1)S(1)}, u32[]{:S(2)}, u32[]{:S(2)}) collective-permute-start(bf16[8,64,256]{2,1,0:T(8,128)(2,1)S(1)} %add_convert_fusion.1), channel_id=1, source_target_pairs={{0,2},{2,0},{4,6},{6,4},{8,10},{10,8},{12,14},{14,12},{16,144},{18... | collective-permute-start | bytes 786440 | tf_op jit(solution)/shard_map/ppermute | solution.py:43
  (8 other events, 228.7 us)
